TPU v7x, 256 devices: a whole 4x4x8 slice. The times are simulated.
256 devices in a mesh: rows: 16 (over x_lo, z), vox: 16 (over x_hi, y, core).
Axes of the slice: x: 4 (x_hi: 2, x_lo: 2; x = x_hi * 2 + x_lo), y: 4, z: 8, core: 2. Of those that a mesh axis runs over, the one named last changes fastest.
Arguments:
- system: float32 [2048, 262144], P('rows', 'vox'), may hold values from -0.01171875 to 0.01171875
- measured: float32 [128, 2048], P(None, 'rows'), may hold values from -18 to 18
- start_image: float32 [128, 262144], P('rows', 'vox'), may hold values from 0 to 1
Outputs:
- image: float32 [128, 262144], P('rows', 'vox')
All inputs are finite; a program needn't handle non-finite values.
Results may differ from a plain program's by a relative error of at most 0.0003.
Values sent between devices are 32-bit elements; how exact they have to be, the bound alone decides.
No kernel may reach another device: no remote copies, remote signals or barrier semaphores. Data moves between devices by JAX's collectives and lax.ppermute only.
A program may use at most 64 MiB of HBM per device.

v0:
```python
import jax
import jax.numpy as jnp
from jax import lax
from jax.sharding import PartitionSpec as P

lower_bound = 0.0
upper_bound = 1.0


def from_everyone(array, axis):
    peers = lax.axis_size(axis)
    return lax.all_to_all(
        jnp.broadcast_to(array[None], (peers, *array.shape)), axis, 0, 0, tiled=True
    )


def of_everyone(array, axis):
    everything = from_everyone(array, axis)
    return jnp.sum(everything, axis=0)


def shifted(block, axis, distance):
    devices = range(lax.axis_size(axis))
    route = [((i - distance) % len(devices), i) for i in devices]
    return lax.ppermute(block, axis, route)


def block_product(current, matrix_tile):
    return lax.dot_general(
        current, matrix_tile, (((1,), (1,)), ((), ())), precision=lax.Precision.HIGHEST
    )


def correct(current, matrix_tile, wanted, summed):
    residual = wanted - summed
    update = jnp.dot(residual, matrix_tile, precision=lax.Precision.HIGHEST)
    return jnp.clip(current + update, lower_bound, upper_bound)


def process(current, matrix_tile, wanted):
    summed = of_everyone(block_product(current, matrix_tile), "vox")
    return correct(current, matrix_tile, wanted, summed)


def shards(system, measured, start_image):
    cycle_size = lax.axis_size("rows")
    position = lax.axis_index("rows")
    frames = start_image.shape[0]

    def visit_image(tick_index, current):
        owner_front = (position - tick_index) % cycle_size
        wanted = lax.dynamic_slice_in_dim(measured, owner_front * frames, frames, 0)
        updated = process(current, system, wanted)
        return shifted(updated, "rows", 1)

    return lax.fori_loop(0, cycle_size, visit_image, start_image)


def solution(mesh):
    placed = (P("rows", "vox"), P(None, "rows"), P("rows", "vox"))
    return jax.shard_map(
        shards, mesh=mesh, in_specs=placed, out_specs=P("rows", "vox"), check_vma=False
    )
```

profile of v0, /device:TPU:1, one launch (start us, length us, event | category | flops | bytes accessed | tf_op | source)
XLA Modules:
  0.0 698.0 jit_solution(8515565192338105480)
XLA Ops:
  1.0 696.1 %while.15 = (s32[]{:T(128)}, f32[8,16384]{1,0:T(8,128)S(1)}, s32[]{:T(128)}, f32[128,128]{1,0:T(8,128)}, f32[128,16384]{1,0:T(8,128)}, /*index=5*/s32[]{:T(128)}...) while((s32[]{:T(128)}, f32[8,16384]{1,0:T(8,128)S(1)}, s32[]{:T(128)}, ...), condition=%wide.region_2.3_spmd, body=%wide.region_0.2_spmd.sunk | while | flops 402931712 | bytes 20795756 | solution.py:56
  1.0 8.9 %fusion.18 = f32[8,128]{1,0:T(8,128)S(1)} fusion(f32[8,16384]{1,0:T(8,128)S(1)} %get-tuple-element.193, f32[128,16384]{1,0:T(8,128)} %get-tuple-element.208), kind=kOutput, calls=%fused_computation.5.clone.1 | convolution fusion | flops 201326592 | bytes 8916992 | tf_op jit(solution)/shard_map/while/body/eval_jaxpr/dot_general | solution.py:29
  10.6 8.4 %all-to-all-start = ((f32[16,8,128]{2,1,0:T(8,128)}), f32[16,8,128]{2,1,0:T(8,128)S(1)}, u32[]{:S(2)}, u32[]{:S(2)}) async-start(f32[16,8,128]{2,1,0:T(8,128)} %broadcast_in_dim.20), calls=%async_computation | async-start | bytes 131072 | tf_op jit(solution)/shard_map/while/body/eval_jaxpr/all_to_all | solution.py:12
  34.5 15.8 %collective-permute-done = f32[8,16384]{1,0:T(8,128)S(1)} collective-permute-done((f32[8,16384]{1,0:T(8,128)S(1)}, f32[8,16384]{1,0:T(8,128)S(1)}, u32[]{:S(2)}, u32[]{:S(2)}) %collective-permute-start) | collective-permute-done | bytes 524320 | tf_op jit(solution)/shard_map/while/body/eval_jaxpr/ppermute | solution.py:25
  50.3 8.9 %fusion.18 = f32[8,128]{1,0:T(8,128)S(1)} fusion(f32[8,16384]{1,0:T(8,128)S(1)} %get-tuple-element.193, f32[128,16384]{1,0:T(8,128)} %get-tuple-element.208), kind=kOutput, calls=%fused_computation.5.clone.1 | convolution fusion | flops 201326592 | bytes 8916992 | tf_op jit(solution)/shard_map/while/body/eval_jaxpr/dot_general | solution.py:29
  64.1 7.4 %all-to-all-done = f32[16,8,128]{2,1,0:T(8,128)S(1)} async-done(((f32[16,8,128]{2,1,0:T(8,128)}), f32[16,8,128]{2,1,0:T(8,128)S(1)}, u32[]{:S(2)}, u32[]{:S(2)}) %all-to-all-start) | async-done | bytes 65568 | tf_op jit(solution)/shard_map/while/body/eval_jaxpr/all_to_all | solution.py:12
  78.0 15.1 %collective-permute-done = f32[8,16384]{1,0:T(8,128)S(1)} collective-permute-done((f32[8,16384]{1,0:T(8,128)S(1)}, f32[8,16384]{1,0:T(8,128)S(1)}, u32[]{:S(2)}, u32[]{:S(2)}) %collective-permute-start) | collective-permute-done | bytes 524320 | tf_op jit(solution)/shard_map/while/body/eval_jaxpr/ppermute | solution.py:25
  93.1 8.9 %fusion.18 = f32[8,128]{1,0:T(8,128)S(1)} fusion(f32[8,16384]{1,0:T(8,128)S(1)} %get-tuple-element.193, f32[128,16384]{1,0:T(8,128)} %get-tuple-element.208), kind=kOutput, calls=%fused_computation.5.clone.1 | convolution fusion | flops 201326592 | bytes 8916992 | tf_op jit(solution)/shard_map/while/body/eval_jaxpr/dot_general | solution.py:29
  107.3 7.4 %all-to-all-done = f32[16,8,128]{2,1,0:T(8,128)S(1)} async-done(((f32[16,8,128]{2,1,0:T(8,128)}), f32[16,8,128]{2,1,0:T(8,128)S(1)}, u32[]{:S(2)}, u32[]{:S(2)}) %all-to-all-start) | async-done | bytes 65568 | tf_op jit(solution)/shard_map/while/body/eval_jaxpr/all_to_all | solution.py:12
  121.2 15.1 %collective-permute-done = f32[8,16384]{1,0:T(8,128)S(1)} collective-permute-done((f32[8,16384]{1,0:T(8,128)S(1)}, f32[8,16384]{1,0:T(8,128)S(1)}, u32[]{:S(2)}, u32[]{:S(2)}) %collective-permute-start) | collective-permute-done | bytes 524320 | tf_op jit(solution)/shard_map/while/body/eval_jaxpr/ppermute | solution.py:25
  136.3 8.9 %fusion.18 = f32[8,128]{1,0:T(8,128)S(1)} fusion(f32[8,16384]{1,0:T(8,128)S(1)} %get-tuple-element.193, f32[128,16384]{1,0:T(8,128)} %get-tuple-element.208), kind=kOutput, calls=%fused_computation.5.clone.1 | convolution fusion | flops 201326592 | bytes 8916992 | tf_op jit(solution)/shard_map/while/body/eval_jaxpr/dot_general | solution.py:29
  150.4 7.4 %all-to-all-done = f32[16,8,128]{2,1,0:T(8,128)S(1)} async-done(((f32[16,8,128]{2,1,0:T(8,128)}), f32[16,8,128]{2,1,0:T(8,128)S(1)}, u32[]{:S(2)}, u32[]{:S(2)}) %all-to-all-start) | async-done | bytes 65568 | tf_op jit(solution)/shard_map/while/body/eval_jaxpr/all_to_all | solution.py:12
  164.3 15.1 %collective-permute-done = f32[8,16384]{1,0:T(8,128)S(1)} collective-permute-done((f32[8,16384]{1,0:T(8,128)S(1)}, f32[8,16384]{1,0:T(8,128)S(1)}, u32[]{:S(2)}, u32[]{:S(2)}) %collective-permute-start) | collective-permute-done | bytes 524320 | tf_op jit(solution)/shard_map/while/body/eval_jaxpr/ppermute | solution.py:25
  179.4 8.9 %fusion.18 = f32[8,128]{1,0:T(8,128)S(1)} fusion(f32[8,16384]{1,0:T(8,128)S(1)} %get-tuple-element.193, f32[128,16384]{1,0:T(8,128)} %get-tuple-element.208), kind=kOutput, calls=%fused_computation.5.clone.1 | convolution fusion | flops 201326592 | bytes 8916992 | tf_op jit(solution)/shard_map/while/body/eval_jaxpr/dot_general | solution.py:29
  193.6 7.4 %all-to-all-done = f32[16,8,128]{2,1,0:T(8,128)S(1)} async-done(((f32[16,8,128]{2,1,0:T(8,128)}), f32[16,8,128]{2,1,0:T(8,128)S(1)}, u32[]{:S(2)}, u32[]{:S(2)}) %all-to-all-start) | async-done | bytes 65568 | tf_op jit(solution)/shard_map/while/body/eval_jaxpr/all_to_all | solution.py:12
  207.4 15.1 %collective-permute-done = f32[8,16384]{1,0:T(8,128)S(1)} collective-permute-done((f32[8,16384]{1,0:T(8,128)S(1)}, f32[8,16384]{1,0:T(8,128)S(1)}, u32[]{:S(2)}, u32[]{:S(2)}) %collective-permute-start) | collective-permute-done | bytes 524320 | tf_op jit(solution)/shard_map/while/body/eval_jaxpr/ppermute | solution.py:25
  222.6 8.9 %fusion.18 = f32[8,128]{1,0:T(8,128)S(1)} fusion(f32[8,16384]{1,0:T(8,128)S(1)} %get-tuple-element.193, f32[128,16384]{1,0:T(8,128)} %get-tuple-element.208), kind=kOutput, calls=%fused_computation.5.clone.1 | convolution fusion | flops 201326592 | bytes 8916992 | tf_op jit(solution)/shard_map/while/body/eval_jaxpr/dot_general | solution.py:29
  236.7 7.4 %all-to-all-done = f32[16,8,128]{2,1,0:T(8,128)S(1)} async-done(((f32[16,8,128]{2,1,0:T(8,128)}), f32[16,8,128]{2,1,0:T(8,128)S(1)}, u32[]{:S(2)}, u32[]{:S(2)}) %all-to-all-start) | async-done | bytes 65568 | tf_op jit(solution)/shard_map/while/body/eval_jaxpr/all_to_all | solution.py:12
  250.6 15.1 %collective-permute-done = f32[8,16384]{1,0:T(8,128)S(1)} collective-permute-done((f32[8,16384]{1,0:T(8,128)S(1)}, f32[8,16384]{1,0:T(8,128)S(1)}, u32[]{:S(2)}, u32[]{:S(2)}) %collective-permute-start) | collective-permute-done | bytes 524320 | tf_op jit(solution)/shard_map/while/body/eval_jaxpr/ppermute | solution.py:25
  265.7 8.9 %fusion.18 = f32[8,128]{1,0:T(8,128)S(1)} fusion(f32[8,16384]{1,0:T(8,128)S(1)} %get-tuple-element.193, f32[128,16384]{1,0:T(8,128)} %get-tuple-element.208), kind=kOutput, calls=%fused_computation.5.clone.1 | convolution fusion | flops 201326592 | bytes 8916992 | tf_op jit(solution)/shard_map/while/body/eval_jaxpr/dot_general | solution.py:29
  279.8 7.4 %all-to-all-done = f32[16,8,128]{2,1,0:T(8,128)S(1)} async-done(((f32[16,8,128]{2,1,0:T(8,128)}), f32[16,8,128]{2,1,0:T(8,128)S(1)}, u32[]{:S(2)}, u32[]{:S(2)}) %all-to-all-start) | async-done | bytes 65568 | tf_op jit(solution)/shard_map/while/body/eval_jaxpr/all_to_all | solution.py:12
  293.7 15.1 %collective-permute-done = f32[8,16384]{1,0:T(8,128)S(1)} collective-permute-done((f32[8,16384]{1,0:T(8,128)S(1)}, f32[8,16384]{1,0:T(8,128)S(1)}, u32[]{:S(2)}, u32[]{:S(2)}) %collective-permute-start) | collective-permute-done | bytes 524320 | tf_op jit(solution)/shard_map/while/body/eval_jaxpr/ppermute | solution.py:25
  308.9 8.9 %fusion.18 = f32[8,128]{1,0:T(8,128)S(1)} fusion(f32[8,16384]{1,0:T(8,128)S(1)} %get-tuple-element.193, f32[128,16384]{1,0:T(8,128)} %get-tuple-element.208), kind=kOutput, calls=%fused_computation.5.clone.1 | convolution fusion | flops 201326592 | bytes 8916992 | tf_op jit(solution)/shard_map/while/body/eval_jaxpr/dot_general | solution.py:29
  323.0 7.4 %all-to-all-done = f32[16,8,128]{2,1,0:T(8,128)S(1)} async-done(((f32[16,8,128]{2,1,0:T(8,128)}), f32[16,8,128]{2,1,0:T(8,128)S(1)}, u32[]{:S(2)}, u32[]{:S(2)}) %all-to-all-start) | async-done | bytes 65568 | tf_op jit(solution)/shard_map/while/body/eval_jaxpr/all_to_all | solution.py:12
  336.9 15.1 %collective-permute-done = f32[8,16384]{1,0:T(8,128)S(1)} collective-permute-done((f32[8,16384]{1,0:T(8,128)S(1)}, f32[8,16384]{1,0:T(8,128)S(1)}, u32[]{:S(2)}, u32[]{:S(2)}) %collective-permute-start) | collective-permute-done | bytes 524320 | tf_op jit(solution)/shard_map/while/body/eval_jaxpr/ppermute | solution.py:25
  352.0 8.9 %fusion.18 = f32[8,128]{1,0:T(8,128)S(1)} fusion(f32[8,16384]{1,0:T(8,128)S(1)} %get-tuple-element.193, f32[128,16384]{1,0:T(8,128)} %get-tuple-element.208), kind=kOutput, calls=%fused_computation.5.clone.1 | convolution fusion | flops 201326592 | bytes 8916992 | tf_op jit(solution)/shard_map/while/body/eval_jaxpr/dot_general | solution.py:29
  366.1 7.4 %all-to-all-done = f32[16,8,128]{2,1,0:T(8,128)S(1)} async-done(((f32[16,8,128]{2,1,0:T(8,128)}), f32[16,8,128]{2,1,0:T(8,128)S(1)}, u32[]{:S(2)}, u32[]{:S(2)}) %all-to-all-start) | async-done | bytes 65568 | tf_op jit(solution)/shard_map/while/body/eval_jaxpr/all_to_all | solution.py:12
  380.0 15.1 %collective-permute-done = f32[8,16384]{1,0:T(8,128)S(1)} collective-permute-done((f32[8,16384]{1,0:T(8,128)S(1)}, f32[8,16384]{1,0:T(8,128)S(1)}, u32[]{:S(2)}, u32[]{:S(2)}) %collective-permute-start) | collective-permute-done | bytes 524320 | tf_op jit(solution)/shard_map/while/body/eval_jaxpr/ppermute | solution.py:25
  395.2 8.9 %fusion.18 = f32[8,128]{1,0:T(8,128)S(1)} fusion(f32[8,16384]{1,0:T(8,128)S(1)} %get-tuple-element.193, f32[128,16384]{1,0:T(8,128)} %get-tuple-element.208), kind=kOutput, calls=%fused_computation.5.clone.1 | convolution fusion | flops 201326592 | bytes 8916992 | tf_op jit(solution)/shard_map/while/body/eval_jaxpr/dot_general | solution.py:29
  409.3 7.4 %all-to-all-done = f32[16,8,128]{2,1,0:T(8,128)S(1)} async-done(((f32[16,8,128]{2,1,0:T(8,128)}), f32[16,8,128]{2,1,0:T(8,128)S(1)}, u32[]{:S(2)}, u32[]{:S(2)}) %all-to-all-start) | async-done | bytes 65568 | tf_op jit(solution)/shard_map/while/body/eval_jaxpr/all_to_all | solution.py:12
  423.2 15.1 %collective-permute-done = f32[8,16384]{1,0:T(8,128)S(1)} collective-permute-done((f32[8,16384]{1,0:T(8,128)S(1)}, f32[8,16384]{1,0:T(8,128)S(1)}, u32[]{:S(2)}, u32[]{:S(2)}) %collective-permute-start) | collective-permute-done | bytes 524320 | tf_op jit(solution)/shard_map/while/body/eval_jaxpr/ppermute | solution.py:25
  438.3 8.9 %fusion.18 = f32[8,128]{1,0:T(8,128)S(1)} fusion(f32[8,16384]{1,0:T(8,128)S(1)} %get-tuple-element.193, f32[128,16384]{1,0:T(8,128)} %get-tuple-element.208), kind=kOutput, calls=%fused_computation.5.clone.1 | convolution fusion | flops 201326592 | bytes 8916992 | tf_op jit(solution)/shard_map/while/body/eval_jaxpr/dot_general | solution.py:29
  452.4 7.4 %all-to-all-done = f32[16,8,128]{2,1,0:T(8,128)S(1)} async-done(((f32[16,8,128]{2,1,0:T(8,128)}), f32[16,8,128]{2,1,0:T(8,128)S(1)}, u32[]{:S(2)}, u32[]{:S(2)}) %all-to-all-start) | async-done | bytes 65568 | tf_op jit(solution)/shard_map/while/body/eval_jaxpr/all_to_all | solution.py:12
  466.3 15.1 %collective-permute-done = f32[8,16384]{1,0:T(8,128)S(1)} collective-permute-done((f32[8,16384]{1,0:T(8,128)S(1)}, f32[8,16384]{1,0:T(8,128)S(1)}, u32[]{:S(2)}, u32[]{:S(2)}) %collective-permute-start) | collective-permute-done | bytes 524320 | tf_op jit(solution)/shard_map/while/body/eval_jaxpr/ppermute | solution.py:25
  481.4 8.9 %fusion.18 = f32[8,128]{1,0:T(8,128)S(1)} fusion(f32[8,16384]{1,0:T(8,128)S(1)} %get-tuple-element.193, f32[128,16384]{1,0:T(8,128)} %get-tuple-element.208), kind=kOutput, calls=%fused_computation.5.clone.1 | convolution fusion | flops 201326592 | bytes 8916992 | tf_op jit(solution)/shard_map/while/body/eval_jaxpr/dot_general | solution.py:29
  495.6 7.4 %all-to-all-done = f32[16,8,128]{2,1,0:T(8,128)S(1)} async-done(((f32[16,8,128]{2,1,0:T(8,128)}), f32[16,8,128]{2,1,0:T(8,128)S(1)}, u32[]{:S(2)}, u32[]{:S(2)}) %all-to-all-start) | async-done | bytes 65568 | tf_op jit(solution)/shard_map/while/body/eval_jaxpr/all_to_all | solution.py:12
  509.5 15.1 %collective-permute-done = f32[8,16384]{1,0:T(8,128)S(1)} collective-permute-done((f32[8,16384]{1,0:T(8,128)S(1)}, f32[8,16384]{1,0:T(8,128)S(1)}, u32[]{:S(2)}, u32[]{:S(2)}) %collective-permute-start) | collective-permute-done | bytes 524320 | tf_op jit(solution)/shard_map/while/body/eval_jaxpr/ppermute | solution.py:25
  524.6 8.9 %fusion.18 = f32[8,128]{1,0:T(8,128)S(1)} fusion(f32[8,16384]{1,0:T(8,128)S(1)} %get-tuple-element.193, f32[128,16384]{1,0:T(8,128)} %get-tuple-element.208), kind=kOutput, calls=%fused_computation.5.clone.1 | convolution fusion | flops 201326592 | bytes 8916992 | tf_op jit(solution)/shard_map/while/body/eval_jaxpr/dot_general | solution.py:29
  538.7 7.4 %all-to-all-done = f32[16,8,128]{2,1,0:T(8,128)S(1)} async-done(((f32[16,8,128]{2,1,0:T(8,128)}), f32[16,8,128]{2,1,0:T(8,128)S(1)}, u32[]{:S(2)}, u32[]{:S(2)}) %all-to-all-start) | async-done | bytes 65568 | tf_op jit(solution)/shard_map/while/body/eval_jaxpr/all_to_all | solution.py:12
  552.6 15.1 %collective-permute-done = f32[8,16384]{1,0:T(8,128)S(1)} collective-permute-done((f32[8,16384]{1,0:T(8,128)S(1)}, f32[8,16384]{1,0:T(8,128)S(1)}, u32[]{:S(2)}, u32[]{:S(2)}) %collective-permute-start) | collective-permute-done | bytes 524320 | tf_op jit(solution)/shard_map/while/body/eval_jaxpr/ppermute | solution.py:25
  567.7 8.9 %fusion.18 = f32[8,128]{1,0:T(8,128)S(1)} fusion(f32[8,16384]{1,0:T(8,128)S(1)} %get-tuple-element.193, f32[128,16384]{1,0:T(8,128)} %get-tuple-element.208), kind=kOutput, calls=%fused_computation.5.clone.1 | convolution fusion | flops 201326592 | bytes 8916992 | tf_op jit(solution)/shard_map/while/body/eval_jaxpr/dot_general | solution.py:29
  581.9 7.4 %all-to-all-done = f32[16,8,128]{2,1,0:T(8,128)S(1)} async-done(((f32[16,8,128]{2,1,0:T(8,128)}), f32[16,8,128]{2,1,0:T(8,128)S(1)}, u32[]{:S(2)}, u32[]{:S(2)}) %all-to-all-start) | async-done | bytes 65568 | tf_op jit(solution)/shard_map/while/body/eval_jaxpr/all_to_all | solution.py:12
  595.7 15.1 %collective-permute-done = f32[8,16384]{1,0:T(8,128)S(1)} collective-permute-done((f32[8,16384]{1,0:T(8,128)S(1)}, f32[8,16384]{1,0:T(8,128)S(1)}, u32[]{:S(2)}, u32[]{:S(2)}) %collective-permute-start) | collective-permute-done | bytes 524320 | tf_op jit(solution)/shard_map/while/body/eval_jaxpr/ppermute | solution.py:25
  610.9 8.9 %fusion.18 = f32[8,128]{1,0:T(8,128)S(1)} fusion(f32[8,16384]{1,0:T(8,128)S(1)} %get-tuple-element.193, f32[128,16384]{1,0:T(8,128)} %get-tuple-element.208), kind=kOutput, calls=%fused_computation.5.clone.1 | convolution fusion | flops 201326592 | bytes 8916992 | tf_op jit(solution)/shard_map/while/body/eval_jaxpr/dot_general | solution.py:29
  638.9 15.1 %collective-permute-done = f32[8,16384]{1,0:T(8,128)S(1)} collective-permute-done((f32[8,16384]{1,0:T(8,128)S(1)}, f32[8,16384]{1,0:T(8,128)S(1)}, u32[]{:S(2)}, u32[]{:S(2)}) %collective-permute-start) | collective-permute-done | bytes 524320 | tf_op jit(solution)/shard_map/while/body/eval_jaxpr/ppermute | solution.py:25
  654.0 8.9 %fusion.18 = f32[8,128]{1,0:T(8,128)S(1)} fusion(f32[8,16384]{1,0:T(8,128)S(1)} %get-tuple-element.193, f32[128,16384]{1,0:T(8,128)} %get-tuple-element.208), kind=kOutput, calls=%fused_computation.5.clone.1 | convolution fusion | flops 201326592 | bytes 8916992 | tf_op jit(solution)/shard_map/while/body/eval_jaxpr/dot_general | solution.py:29
  668.1 7.4 %all-to-all-done = f32[16,8,128]{2,1,0:T(8,128)S(1)} async-done(((f32[16,8,128]{2,1,0:T(8,128)}), f32[16,8,128]{2,1,0:T(8,128)S(1)}, u32[]{:S(2)}, u32[]{:S(2)}) %all-to-all-start) | async-done | bytes 65568 | tf_op jit(solution)/shard_map/while/body/eval_jaxpr/all_to_all | solution.py:12
  682.0 15.1 %collective-permute-done = f32[8,16384]{1,0:T(8,128)S(1)} collective-permute-done((f32[8,16384]{1,0:T(8,128)S(1)}, f32[8,16384]{1,0:T(8,128)S(1)}, u32[]{:S(2)}, u32[]{:S(2)}) %collective-permute-start) | collective-permute-done | bytes 524320 | tf_op jit(solution)/shard_map/while/body/eval_jaxpr/ppermute | solution.py:25
  (83 shorter events, 200.7 us)
Async XLA Ops:
  10.6 15.8 %all-to-all-start = ((f32[16,8,128]{2,1,0:T(8,128)}), f32[16,8,128]{2,1,0:T(8,128)S(1)}, u32[]{:S(2)}, u32[]{:S(2)}) async-start(f32[16,8,128]{2,1,0:T(8,128)} %broadcast_in_dim.20), calls=%async_computation | async-start | bytes 131072 | tf_op jit(solution)/shard_map/while/body/eval_jaxpr/all_to_all | solution.py:12
  32.7 17.5 %collective-permute-start = (f32[8,16384]{1,0:T(8,128)S(1)}, f32[8,16384]{1,0:T(8,128)S(1)}, u32[]{:S(2)}, u32[]{:S(2)}) collective-permute-start(f32[8,16384]{1,0:T(8,128)S(1)} %fusion.19), channel_id=1, source_target_pairs={{240,0},{0,16},{16,32},{32,48},{48,64},{64,80},{80,96},{96,112},{1... | collective-permute-start | bytes 1572872 | tf_op jit(solution)/shard_map/while/body/eval_jaxpr/ppermute | solution.py:25
  59.8 11.7 %all-to-all-start = ((f32[16,8,128]{2,1,0:T(8,128)}), f32[16,8,128]{2,1,0:T(8,128)S(1)}, u32[]{:S(2)}, u32[]{:S(2)}) async-start(f32[16,8,128]{2,1,0:T(8,128)} %broadcast_in_dim.20), calls=%async_computation | async-start | bytes 131072 | tf_op jit(solution)/shard_map/while/body/eval_jaxpr/all_to_all | solution.py:12
  77.9 15.2 %collective-permute-start = (f32[8,16384]{1,0:T(8,128)S(1)}, f32[8,16384]{1,0:T(8,128)S(1)}, u32[]{:S(2)}, u32[]{:S(2)}) collective-permute-start(f32[8,16384]{1,0:T(8,128)S(1)} %fusion.19), channel_id=1, source_target_pairs={{240,0},{0,16},{16,32},{32,48},{48,64},{64,80},{80,96},{96,112},{1... | collective-permute-start | bytes 1572872 | tf_op jit(solution)/shard_map/while/body/eval_jaxpr/ppermute | solution.py:25
  102.7 12.0 %all-to-all-start = ((f32[16,8,128]{2,1,0:T(8,128)}), f32[16,8,128]{2,1,0:T(8,128)S(1)}, u32[]{:S(2)}, u32[]{:S(2)}) async-start(f32[16,8,128]{2,1,0:T(8,128)} %broadcast_in_dim.20), calls=%async_computation | async-start | bytes 131072 | tf_op jit(solution)/shard_map/while/body/eval_jaxpr/all_to_all | solution.py:12
  121.1 15.2 %collective-permute-start = (f32[8,16384]{1,0:T(8,128)S(1)}, f32[8,16384]{1,0:T(8,128)S(1)}, u32[]{:S(2)}, u32[]{:S(2)}) collective-permute-start(f32[8,16384]{1,0:T(8,128)S(1)} %fusion.19), channel_id=1, source_target_pairs={{240,0},{0,16},{16,32},{32,48},{48,64},{64,80},{80,96},{96,112},{1... | collective-permute-start | bytes 1572872 | tf_op jit(solution)/shard_map/while/body/eval_jaxpr/ppermute | solution.py:25
  145.8 12.0 %all-to-all-start = ((f32[16,8,128]{2,1,0:T(8,128)}), f32[16,8,128]{2,1,0:T(8,128)S(1)}, u32[]{:S(2)}, u32[]{:S(2)}) async-start(f32[16,8,128]{2,1,0:T(8,128)} %broadcast_in_dim.20), calls=%async_computation | async-start | bytes 131072 | tf_op jit(solution)/shard_map/while/body/eval_jaxpr/all_to_all | solution.py:12
  164.2 15.2 %collective-permute-start = (f32[8,16384]{1,0:T(8,128)S(1)}, f32[8,16384]{1,0:T(8,128)S(1)}, u32[]{:S(2)}, u32[]{:S(2)}) collective-permute-start(f32[8,16384]{1,0:T(8,128)S(1)} %fusion.19), channel_id=1, source_target_pairs={{240,0},{0,16},{16,32},{32,48},{48,64},{64,80},{80,96},{96,112},{1... | collective-permute-start | bytes 1572872 | tf_op jit(solution)/shard_map/while/body/eval_jaxpr/ppermute | solution.py:25
  189.0 12.0 %all-to-all-start = ((f32[16,8,128]{2,1,0:T(8,128)}), f32[16,8,128]{2,1,0:T(8,128)S(1)}, u32[]{:S(2)}, u32[]{:S(2)}) async-start(f32[16,8,128]{2,1,0:T(8,128)} %broadcast_in_dim.20), calls=%async_computation | async-start | bytes 131072 | tf_op jit(solution)/shard_map/while/body/eval_jaxpr/all_to_all | solution.py:12
  207.3 15.2 %collective-permute-start = (f32[8,16384]{1,0:T(8,128)S(1)}, f32[8,16384]{1,0:T(8,128)S(1)}, u32[]{:S(2)}, u32[]{:S(2)}) collective-permute-start(f32[8,16384]{1,0:T(8,128)S(1)} %fusion.19), channel_id=1, source_target_pairs={{240,0},{0,16},{16,32},{32,48},{48,64},{64,80},{80,96},{96,112},{1... | collective-permute-start | bytes 1572872 | tf_op jit(solution)/shard_map/while/body/eval_jaxpr/ppermute | solution.py:25
  232.1 12.0 %all-to-all-start = ((f32[16,8,128]{2,1,0:T(8,128)}), f32[16,8,128]{2,1,0:T(8,128)S(1)}, u32[]{:S(2)}, u32[]{:S(2)}) async-start(f32[16,8,128]{2,1,0:T(8,128)} %broadcast_in_dim.20), calls=%async_computation | async-start | bytes 131072 | tf_op jit(solution)/shard_map/while/body/eval_jaxpr/all_to_all | solution.py:12
  250.5 15.2 %collective-permute-start = (f32[8,16384]{1,0:T(8,128)S(1)}, f32[8,16384]{1,0:T(8,128)S(1)}, u32[]{:S(2)}, u32[]{:S(2)}) collective-permute-start(f32[8,16384]{1,0:T(8,128)S(1)} %fusion.19), channel_id=1, source_target_pairs={{240,0},{0,16},{16,32},{32,48},{48,64},{64,80},{80,96},{96,112},{1... | collective-permute-start | bytes 1572872 | tf_op jit(solution)/shard_map/while/body/eval_jaxpr/ppermute | solution.py:25
  275.3 12.0 %all-to-all-start = ((f32[16,8,128]{2,1,0:T(8,128)}), f32[16,8,128]{2,1,0:T(8,128)S(1)}, u32[]{:S(2)}, u32[]{:S(2)}) async-start(f32[16,8,128]{2,1,0:T(8,128)} %broadcast_in_dim.20), calls=%async_computation | async-start | bytes 131072 | tf_op jit(solution)/shard_map/while/body/eval_jaxpr/all_to_all | solution.py:12
  293.6 15.2 %collective-permute-start = (f32[8,16384]{1,0:T(8,128)S(1)}, f32[8,16384]{1,0:T(8,128)S(1)}, u32[]{:S(2)}, u32[]{:S(2)}) collective-permute-start(f32[8,16384]{1,0:T(8,128)S(1)} %fusion.19), channel_id=1, source_target_pairs={{240,0},{0,16},{16,32},{32,48},{48,64},{64,80},{80,96},{96,112},{1... | collective-permute-start | bytes 1572872 | tf_op jit(solution)/shard_map/while/body/eval_jaxpr/ppermute | solution.py:25
  318.4 12.0 %all-to-all-start = ((f32[16,8,128]{2,1,0:T(8,128)}), f32[16,8,128]{2,1,0:T(8,128)S(1)}, u32[]{:S(2)}, u32[]{:S(2)}) async-start(f32[16,8,128]{2,1,0:T(8,128)} %broadcast_in_dim.20), calls=%async_computation | async-start | bytes 131072 | tf_op jit(solution)/shard_map/while/body/eval_jaxpr/all_to_all | solution.py:12
  336.8 15.2 %collective-permute-start = (f32[8,16384]{1,0:T(8,128)S(1)}, f32[8,16384]{1,0:T(8,128)S(1)}, u32[]{:S(2)}, u32[]{:S(2)}) collective-permute-start(f32[8,16384]{1,0:T(8,128)S(1)} %fusion.19), channel_id=1, source_target_pairs={{240,0},{0,16},{16,32},{32,48},{48,64},{64,80},{80,96},{96,112},{1... | collective-permute-start | bytes 1572872 | tf_op jit(solution)/shard_map/while/body/eval_jaxpr/ppermute | solution.py:25
  361.5 12.0 %all-to-all-start = ((f32[16,8,128]{2,1,0:T(8,128)}), f32[16,8,128]{2,1,0:T(8,128)S(1)}, u32[]{:S(2)}, u32[]{:S(2)}) async-start(f32[16,8,128]{2,1,0:T(8,128)} %broadcast_in_dim.20), calls=%async_computation | async-start | bytes 131072 | tf_op jit(solution)/shard_map/while/body/eval_jaxpr/all_to_all | solution.py:12
  379.9 15.2 %collective-permute-start = (f32[8,16384]{1,0:T(8,128)S(1)}, f32[8,16384]{1,0:T(8,128)S(1)}, u32[]{:S(2)}, u32[]{:S(2)}) collective-permute-start(f32[8,16384]{1,0:T(8,128)S(1)} %fusion.19), channel_id=1, source_target_pairs={{240,0},{0,16},{16,32},{32,48},{48,64},{64,80},{80,96},{96,112},{1... | collective-permute-start | bytes 1572872 | tf_op jit(solution)/shard_map/while/body/eval_jaxpr/ppermute | solution.py:25
  404.7 12.0 %all-to-all-start = ((f32[16,8,128]{2,1,0:T(8,128)}), f32[16,8,128]{2,1,0:T(8,128)S(1)}, u32[]{:S(2)}, u32[]{:S(2)}) async-start(f32[16,8,128]{2,1,0:T(8,128)} %broadcast_in_dim.20), calls=%async_computation | async-start | bytes 131072 | tf_op jit(solution)/shard_map/while/body/eval_jaxpr/all_to_all | solution.py:12
  423.1 15.2 %collective-permute-start = (f32[8,16384]{1,0:T(8,128)S(1)}, f32[8,16384]{1,0:T(8,128)S(1)}, u32[]{:S(2)}, u32[]{:S(2)}) collective-permute-start(f32[8,16384]{1,0:T(8,128)S(1)} %fusion.19), channel_id=1, source_target_pairs={{240,0},{0,16},{16,32},{32,48},{48,64},{64,80},{80,96},{96,112},{1... | collective-permute-start | bytes 1572872 | tf_op jit(solution)/shard_map/while/body/eval_jaxpr/ppermute | solution.py:25
  447.8 12.0 %all-to-all-start = ((f32[16,8,128]{2,1,0:T(8,128)}), f32[16,8,128]{2,1,0:T(8,128)S(1)}, u32[]{:S(2)}, u32[]{:S(2)}) async-start(f32[16,8,128]{2,1,0:T(8,128)} %broadcast_in_dim.20), calls=%async_computation | async-start | bytes 131072 | tf_op jit(solution)/shard_map/while/body/eval_jaxpr/all_to_all | solution.py:12
  466.2 15.2 %collective-permute-start = (f32[8,16384]{1,0:T(8,128)S(1)}, f32[8,16384]{1,0:T(8,128)S(1)}, u32[]{:S(2)}, u32[]{:S(2)}) collective-permute-start(f32[8,16384]{1,0:T(8,128)S(1)} %fusion.19), channel_id=1, source_target_pairs={{240,0},{0,16},{16,32},{32,48},{48,64},{64,80},{80,96},{96,112},{1... | collective-permute-start | bytes 1572872 | tf_op jit(solution)/shard_map/while/body/eval_jaxpr/ppermute | solution.py:25
  491.0 12.0 %all-to-all-start = ((f32[16,8,128]{2,1,0:T(8,128)}), f32[16,8,128]{2,1,0:T(8,128)S(1)}, u32[]{:S(2)}, u32[]{:S(2)}) async-start(f32[16,8,128]{2,1,0:T(8,128)} %broadcast_in_dim.20), calls=%async_computation | async-start | bytes 131072 | tf_op jit(solution)/shard_map/while/body/eval_jaxpr/all_to_all | solution.py:12
  509.4 15.2 %collective-permute-start = (f32[8,16384]{1,0:T(8,128)S(1)}, f32[8,16384]{1,0:T(8,128)S(1)}, u32[]{:S(2)}, u32[]{:S(2)}) collective-permute-start(f32[8,16384]{1,0:T(8,128)S(1)} %fusion.19), channel_id=1, source_target_pairs={{240,0},{0,16},{16,32},{32,48},{48,64},{64,80},{80,96},{96,112},{1... | collective-permute-start | bytes 1572872 | tf_op jit(solution)/shard_map/while/body/eval_jaxpr/ppermute | solution.py:25
  534.1 12.0 %all-to-all-start = ((f32[16,8,128]{2,1,0:T(8,128)}), f32[16,8,128]{2,1,0:T(8,128)S(1)}, u32[]{:S(2)}, u32[]{:S(2)}) async-start(f32[16,8,128]{2,1,0:T(8,128)} %broadcast_in_dim.20), calls=%async_computation | async-start | bytes 131072 | tf_op jit(solution)/shard_map/while/body/eval_jaxpr/all_to_all | solution.py:12
  552.5 15.2 %collective-permute-start = (f32[8,16384]{1,0:T(8,128)S(1)}, f32[8,16384]{1,0:T(8,128)S(1)}, u32[]{:S(2)}, u32[]{:S(2)}) collective-permute-start(f32[8,16384]{1,0:T(8,128)S(1)} %fusion.19), channel_id=1, source_target_pairs={{240,0},{0,16},{16,32},{32,48},{48,64},{64,80},{80,96},{96,112},{1... | collective-permute-start | bytes 1572872 | tf_op jit(solution)/shard_map/while/body/eval_jaxpr/ppermute | solution.py:25
  577.3 12.0 %all-to-all-start = ((f32[16,8,128]{2,1,0:T(8,128)}), f32[16,8,128]{2,1,0:T(8,128)S(1)}, u32[]{:S(2)}, u32[]{:S(2)}) async-start(f32[16,8,128]{2,1,0:T(8,128)} %broadcast_in_dim.20), calls=%async_computation | async-start | bytes 131072 | tf_op jit(solution)/shard_map/while/body/eval_jaxpr/all_to_all | solution.py:12
  595.6 15.2 %collective-permute-start = (f32[8,16384]{1,0:T(8,128)S(1)}, f32[8,16384]{1,0:T(8,128)S(1)}, u32[]{:S(2)}, u32[]{:S(2)}) collective-permute-start(f32[8,16384]{1,0:T(8,128)S(1)} %fusion.19), channel_id=1, source_target_pairs={{240,0},{0,16},{16,32},{32,48},{48,64},{64,80},{80,96},{96,112},{1... | collective-permute-start | bytes 1572872 | tf_op jit(solution)/shard_map/while/body/eval_jaxpr/ppermute | solution.py:25
  620.4 12.0 %all-to-all-start = ((f32[16,8,128]{2,1,0:T(8,128)}), f32[16,8,128]{2,1,0:T(8,128)S(1)}, u32[]{:S(2)}, u32[]{:S(2)}) async-start(f32[16,8,128]{2,1,0:T(8,128)} %broadcast_in_dim.20), calls=%async_computation | async-start | bytes 131072 | tf_op jit(solution)/shard_map/while/body/eval_jaxpr/all_to_all | solution.py:12
  638.8 15.2 %collective-permute-start = (f32[8,16384]{1,0:T(8,128)S(1)}, f32[8,16384]{1,0:T(8,128)S(1)}, u32[]{:S(2)}, u32[]{:S(2)}) collective-permute-start(f32[8,16384]{1,0:T(8,128)S(1)} %fusion.19), channel_id=1, source_target_pairs={{240,0},{0,16},{16,32},{32,48},{48,64},{64,80},{80,96},{96,112},{1... | collective-permute-start | bytes 1572872 | tf_op jit(solution)/shard_map/while/body/eval_jaxpr/ppermute | solution.py:25
  663.6 12.0 %all-to-all-start = ((f32[16,8,128]{2,1,0:T(8,128)}), f32[16,8,128]{2,1,0:T(8,128)S(1)}, u32[]{:S(2)}, u32[]{:S(2)}) async-start(f32[16,8,128]{2,1,0:T(8,128)} %broadcast_in_dim.20), calls=%async_computation | async-start | bytes 131072 | tf_op jit(solution)/shard_map/while/body/eval_jaxpr/all_to_all | solution.py:12
  681.9 15.2 %collective-permute-start = (f32[8,16384]{1,0:T(8,128)S(1)}, f32[8,16384]{1,0:T(8,128)S(1)}, u32[]{:S(2)}, u32[]{:S(2)}) collective-permute-start(f32[8,16384]{1,0:T(8,128)S(1)} %fusion.19), channel_id=1, source_target_pairs={{240,0},{0,16},{16,32},{32,48},{48,64},{64,80},{80,96},{96,112},{1... | collective-permute-start | bytes 1572872 | tf_op jit(solution)/shard_map/while/body/eval_jaxpr/ppermute | solution.py:25
where the time goes:
time: 699 us; the launch traced here: 698 us
  waiting for transfers between devices  361 us (52%)
  matrix products  244 us (35%)
  starting transfers between devices  79.9 us (11%)
  local copies, waits for them, and re-layouts  12.3 us (2%)
    ppermute x16, waiting for transfers between devices, shifted(): return lax.ppermute(block, axis, route)  243 us
    dot_general x16, matrix products, block_product(): lax.dot_general(current, matrix_tile, (((1,), (1,)), ((), ())), precision...  142 us
    all_to_all x16, waiting for transfers between devices, from_everyone(): lax.all_to_all(jnp.broadcast_to(array[None], (peers, *array.shape)), axis...  118 us
    dot_general x16, matrix products, correct(): update = jnp.dot(residual, matrix_tile, precision=lax.Precision.HIGHEST)  102 us
    all_to_all x16, starting transfers between devices, from_everyone(): lax.all_to_all(jnp.broadcast_to(array[None], (peers, *array.shape)), axis...  76.9 us
  transfers between devices with their start and end apart: 32, of which 32 were waited for; matrix products, arithmetic and copies ran while one was open for 0% of the time, Pallas kernels for 0%

commit v1 on v0

v1 whole, which is shorter than its diff:
```python
import functools

import jax
import jax.numpy as jnp
from jax import lax
from jax.experimental import pallas as pl
from jax.experimental.pallas import tpu as pltpu
from jax.sharding import PartitionSpec as P


lower_bound = 0.0
upper_bound = 1.0

CHUNK = 2048
f32 = jnp.float32
bf16 = jnp.bfloat16
VMEM = pl.BlockSpec(memory_space=pltpu.VMEM)
SMEM = pl.BlockSpec(memory_space=pltpu.SMEM)

HELD = (0, 1, 2, 3, 4, 5, 6, 7, 8, 8, 8, 8, 8, 8, 8, 8)

barrier = lax.optimization_barrier


def gate(value, *others):
    return barrier((value, *others))[0]


def parts_of(value):
    hi = value.astype(bf16)
    return hi, (value - hi.astype(f32)).astype(bf16)


def split_kernel(a_ref, o_ref, *refs):
    sems, copies = refs[-1], refs[:-1]
    moves = [
        pltpu.make_async_copy(a_ref.at[:, pl.ds(c * CHUNK, CHUNK)], copy, sems.at[c])
        for c, copy in enumerate(copies)
    ]
    for move in moves:
        move.start()

    def step(c, _):
        o_ref[c] = jnp.concatenate(parts_of(a_ref[:, at(c)]), axis=0)
        return 0

    lax.fori_loop(0, o_ref.shape[0], step, 0)
    for move in moves:
        move.wait()


def split_rows(system):
    rows, vox = system.shape
    n = vox // CHUNK
    own, *copies = pl.pallas_call(
        split_kernel,
        in_specs=[VMEM],
        out_specs=[VMEM] + [pl.BlockSpec(memory_space=pl.ANY)] * n,
        out_shape=[jax.ShapeDtypeStruct((n, 2 * rows, CHUNK), bf16)]
        + [jax.ShapeDtypeStruct((rows, CHUNK), f32)] * n,
        scratch_shapes=[pltpu.SemaphoreType.DMA((n,))],
        compiler_params=pltpu.CompilerParams(vmem_limit_bytes=8 << 20),
        name="split_rows",
    )(system)
    return own, copies


def arrange_kernel(front_ref, meas_ref, o_ref):
    for k in range(o_ref.shape[0]):
        f = front_ref[k]
        o_ref[k] = meas_ref[pl.ds(pl.multiple_of(f * 8, 8), 8), :]


def arranged(measured, fronts):
    n = fronts.shape[0]
    return pl.pallas_call(
        arrange_kernel,
        in_specs=[SMEM, VMEM],
        out_specs=VMEM,
        out_shape=jax.ShapeDtypeStruct((n, measured.shape[0] // n, measured.shape[1]), f32),
        name="arranged",
    )(fronts, measured)


def turn_kernel(a_ref, *refs):
    o_ref = refs[-1]
    hi, lo = parts_of(a_ref[...])
    o_ref[0] = jnp.concatenate([hi.astype(f32).T.astype(bf16), lo.astype(f32).T.astype(bf16)], axis=1)


def split_turned(index, chunk, store):
    rows = chunk.shape[0]
    shape = (8, CHUNK, 2 * rows) if store is None else store.shape
    operands = [chunk] if store is None else [chunk, store]
    return pl.pallas_call(
        turn_kernel,
        grid=(1,),
        in_specs=[
            pl.BlockSpec(chunk.shape, lambda i: (0, 0)),
            pl.BlockSpec(memory_space=pl.ANY),
        ][: len(operands)],
        out_specs=pl.BlockSpec((1, *shape[1:]), lambda i: (index, 0, 0)),
        out_shape=jax.ShapeDtypeStruct(shape, bf16),
        input_output_aliases={} if store is None else {1: 0},
        compiler_params=pltpu.CompilerParams(vmem_limit_bytes=8 << 20),
        cost_estimate=pl.CostEstimate(flops=1 << 20, bytes_accessed=2 << 20, transcendentals=0),
        name="split_turned",
    )(*operands)


def at(c):
    return pl.ds(pl.multiple_of(c * CHUNK, CHUNK), CHUNK)


def product_kernel(first, turned, add, *refs):
    x_ref, a_ref = refs[0], refs[1]
    o_ref, acc = refs[-2], refs[-1]
    acc[...] = jnp.zeros_like(acc)

    def step(c, _):
        lhs = jnp.concatenate(parts_of(x_ref[:, at(c)]), axis=0)
        if turned:
            acc[...] += jnp.dot(lhs, a_ref[c + first], preferred_element_type=f32)
        else:
            acc[...] += lax.dot_general(
                lhs, a_ref[c + first], (((1,), (1,)), ((), ())), preferred_element_type=f32
            )
        return 0

    lax.fori_loop(0, x_ref.shape[1] // CHUNK, step, 0)
    both = acc[0:8, :] + acc[8:16, :]
    p = both[:, :128] + both[:, 128:]
    o_ref[...] = p + refs[2][...] if add else p


def product(x, a, first, turned, before):
    operands = [x, a] + ([] if before is None else [before])
    return pl.pallas_call(
        functools.partial(product_kernel, first, turned, before is not None),
        in_specs=[VMEM] * len(operands),
        out_specs=VMEM,
        out_shape=jax.ShapeDtypeStruct((8, 128), f32),
        scratch_shapes=[pltpu.VMEM((16, 256), f32)],
        compiler_params=pltpu.CompilerParams(vmem_limit_bytes=4 << 20),
        cost_estimate=pl.CostEstimate(flops=1 << 28, bytes_accessed=4 << 20, transcendentals=0),
        name="product",
    )(*operands)


def update_kernel(k, ins, outs, total_ref, wanted_ref, a_ref, *refs):
    one = jnp.concatenate(parts_of(wanted_ref[k] - total_ref[...]), axis=0)
    lhs = jnp.concatenate([one, one], axis=1)
    cuts = sorted({0, *ins, *outs})

    def piece(sizes, c):
        begin = 0
        for i, end in enumerate(sizes):
            if c < end:
                return i, begin
            begin = end

    for low, high in zip(cuts[:-1], cuts[1:]):
        i, i0 = piece(ins, low)
        o, o0 = piece(outs, low)
        x_ref, o_ref = refs[i], refs[len(ins) + o]

        def step(c, _):
            d = jnp.dot(lhs, a_ref[c], preferred_element_type=f32)
            x = x_ref[:, at(c - i0)] + (d[0:8] + d[8:16])
            o_ref[:, at(c - o0)] = jnp.clip(x, lower_bound, upper_bound)
            return 0

        lax.fori_loop(low, high, step, 0)


def update(k, total, wanted, a, pieces, ins, outs):
    sizes = [e - b for b, e in zip((0, *outs[:-1]), outs)]
    return pl.pallas_call(
        functools.partial(update_kernel, k, ins, outs),
        in_specs=[VMEM] * (3 + len(pieces)),
        out_specs=[VMEM] * len(outs),
        out_shape=[jax.ShapeDtypeStruct((8, n * CHUNK), f32) for n in sizes],
        compiler_params=pltpu.CompilerParams(vmem_limit_bytes=4 << 20),
        cost_estimate=pl.CostEstimate(flops=1 << 28, bytes_accessed=4 << 20, transcendentals=0),
        name="update",
    )(total, wanted, a, *pieces)


def shifted(block, distance):
    n = lax.axis_size("rows")
    return lax.ppermute(block, "rows", [(i, (i + distance) % n) for i in range(n)])


def exchanged(p, reach):
    n = lax.axis_size("vox")
    return p + lax.ppermute(p, "vox", [(i, i ^ reach) for i in range(n)])


def ends(held, n):
    return tuple(e for e in (held, n) if e > 0) if held < n else (n,)


def shards(system, measured, start_image):
    cycle = lax.axis_size("rows")
    position = lax.axis_index("rows")
    n = system.shape[1] // CHUNK
    fronts = ((position - jnp.arange(cycle)) % cycle).astype(jnp.int32)
    wanted = arranged(measured, fronts)
    own, chunks = split_rows(system)
    arriving = []
    following = None
    pieces, ins, held = [start_image], (n,), 0
    p = product(start_image, own, 0, False, None)
    for k in range(cycle):
        last = k == cycle - 1
        now = 0 if last else HELD[k]
        outs = ends(now, n)
        p = exchanged(p, 8)
        if len(arriving) < n and not last:
            p, chunk = barrier((p, chunks[len(arriving)]))
            arriving.append(shifted(chunk, -1))
        p = exchanged(p, 1)
        for reach in (2, 4):
            p = exchanged(p, reach)
        new = update(k, p, wanted, own, pieces, ins, outs)
        if last:
            return shifted(new[0], 1)
        if now < n:
            far = shifted(new[-1], 1)
        for c in range(held, now):
            following = split_turned(c, gate(arriving[c], p), following)
        held = now
        if now == 0:
            pieces = [far]
            p = product(far, own, 0, False, None)
        else:
            p = product(new[0], following, 0, True, None)
            p, kept = barrier((p, new[0]))
            p = shifted(p, 1)
            near = shifted(kept, 1)
            if now < n:
                p = product(far, own, now, False, p)
                pieces = [near, far]
            else:
                pieces = [near]
        ins = outs


def solution(mesh):
    placed = (P("rows", "vox"), P(None, "rows"), P("rows", "vox"))
    return jax.shard_map(
        shards, mesh=mesh, in_specs=placed, out_specs=P("rows", "vox"), check_vma=False
    )
```

time: 699 us -> 547 us (0.78); the launches traced: 698 us -> 537 us
  matrix products: 244 us -> 0 us
  Pallas kernels: 0 us -> 77.2 us
  starting transfers between devices: 79.9 us -> 156 us
  waiting for transfers between devices: 361 us -> 290 us
    dot_general x32 -> x0, matrix products: 244 us -> none  [the longest x16 142 us: block_product(): lax.dot_general(current, matrix_tile, (((1,), (1,)), ((), ())), precision...]
    ppermute x16 -> x109, starting transfers between devices: 2.97 us -> 156 us  [the longest x64 135 us: exchanged(): return p + lax.ppermute(p, 'vox', [(i, i ^ reach) for i in range(n)])]
    all_to_all x16 -> x0, waiting for transfers between devices: 118 us -> none  [from_everyone(): lax.all_to_all(jnp.broadcast_to(array[None], (peers, *array.shape)), axis...]
    pallas_call x0 -> x49, Pallas kernels: none -> 77.2 us  [the longest x23 38.9 us: product(): pl.pallas_call(functools.partial(product_kernel, first, turned, before is...]
    all_to_all x16 -> x0, starting transfers between devices: 76.9 us -> none  [from_everyone(): lax.all_to_all(jnp.broadcast_to(array[None], (peers, *array.shape)), axis...]
    ppermute x16 -> x109, waiting for transfers between devices: 243 us -> 290 us  [the longest x45 170 us: shifted(): lax.ppermute(block, 'rows', [(i, (i + distance) % n) for i in range(n)])]
    broadcast_in_dim x16 -> x0, local copies, waits for them, and re-layouts: 10.5 us -> none  [from_everyone(): jnp.broadcast_to(array[None], (peers, *array.shape))]
    unnamed x2 -> x37, local copies, waits for them, and re-layouts: 1.83 us -> 11.8 us
  transfers between devices with their start and end apart: 32 -> 109, of which waited for: 32 -> 86; matrix products, arithmetic and copies ran while one was open for 0% -> 0% of each run, Pallas kernels for 0% -> 8%
where the time goes in v1:
time: 547 us; the launch traced here: 537 us
  waiting for transfers between devices  290 us (53%)
  starting transfers between devices  156 us (29%)
  Pallas kernels  77.2 us (14%)
  local copies, waits for them, and re-layouts  11.8 us (2%)
    ppermute x45, waiting for transfers between devices, shifted(): lax.ppermute(block, 'rows', [(i, (i + distance) % n) for i in range(n)])  170 us
    ppermute x64, starting transfers between devices, exchanged(): return p + lax.ppermute(p, 'vox', [(i, i ^ reach) for i in range(n)])  135 us
    ppermute x64, waiting for transfers between devices, exchanged(): return p + lax.ppermute(p, 'vox', [(i, i ^ reach) for i in range(n)])  119 us
    pallas_call x23, Pallas kernels, product(): pl.pallas_call(functools.partial(product_kernel, first, turned, before is...  38.9 us
    pallas_call x16, Pallas kernels, update(): pl.pallas_call(functools.partial(update_kernel, k, ins, outs), in_specs=[...  32.2 us
    ppermute x45, starting transfers between devices, shifted(): lax.ppermute(block, 'rows', [(i, (i + distance) % n) for i in range(n)])  21.5 us
    unnamed x37, local copies, waits for them, and re-layouts  11.8 us
  transfers between devices with their start and end apart: 109, of which 86 were waited for; matrix products, arithmetic and copies ran while one was open for 0% of the time, Pallas kernels for 8%

profile of v1, /device:TPU:1, one launch (start us, length us, event | category | flops | bytes accessed | tf_op | source)
XLA Modules:
  0.0 536.8 jit_solution(17704232777312159024)
XLA Ops:
  0.0 3.4 copy-done.5
  5.3 3.1 product.23
  8.4 3.3 copy-done
  11.7 3.6 collective-permute-start
  16.3 3.8 collective-permute-start.1
  27.5 3.4 copy-done.1
  34.7 5.0 collective-permute-start.10
  39.7 10.4 %collective-permute-done.4.refs_0_ = f32[8,16384]{1,0:T(8,128)S(1)} collective-permute-done((f32[8,16384]{1,0:T(8,128)S(1)}, f32[8,16384]{1,0:T(8,128)S(1)}, u32[]{:S(2)}, u32[]{:S(2)}) %collective-permute-start.4) | collective-permute-done | bytes 524320 | tf_op jit(solution)/shard_map/ppermute | solution.py:191
  50.1 3.1 product.24
  59.2 3.7 collective-permute-start.6
  73.2 11.2 %collective-permute-done.9.refs_0_.refs_1_ = f32[8,14336]{1,0:T(8,128)S(1)} collective-permute-done((f32[8,14336]{1,0:T(8,128)S(1)}, f32[8,14336]{1,0:T(8,128)S(1)}, u32[]{:S(2)}, u32[]{:S(2)}) %collective-permute-start.9) | collective-permute-done | bytes 458784 | tf_op jit(solution)/shard_map/ppermute | solution.py:191
  84.5 2.7 product.26
  93.8 4.0 collective-permute-start.13
  108.3 9.5 %collective-permute-done.17.refs_0_.refs_1_ = f32[8,12288]{1,0:T(8,128)S(1)} collective-permute-done((f32[8,12288]{1,0:T(8,128)S(1)}, f32[8,12288]{1,0:T(8,128)S(1)}, u32[]{:S(2)}, u32[]{:S(2)}) %collective-permute-start.17) | collective-permute-done | bytes 393248 | tf_op jit(solution)/shard_map/ppermute | solution.py:191
  121.0 3.3 collective-permute-done.20
  125.8 4.9 collective-permute-start.21
  141.6 7.8 %collective-permute-done.25.refs_0_.refs_1_ = f32[8,10240]{1,0:T(8,128)S(1)} collective-permute-done((f32[8,10240]{1,0:T(8,128)S(1)}, f32[8,10240]{1,0:T(8,128)S(1)}, u32[]{:S(2)}, u32[]{:S(2)}) %collective-permute-start.25) | collective-permute-done | bytes 327712 | tf_op jit(solution)/shard_map/ppermute | solution.py:191
  152.2 3.3 collective-permute-done.28
  156.1 4.4 collective-permute-start.29
  173.2 4.2 collective-permute-done.33.refs_0_.refs_1_
  185.2 5.2 collective-permute-start.37
  201.8 4.9 collective-permute-done.41.refs_0_.refs_1_
  213.3 4.9 collective-permute-start.45
  230.4 3.4 collective-permute-done.49.refs_0_.refs_1_
  241.2 5.5 %collective-permute-start.53 = (f32[8,128]{1,0:T(8,128)S(1)}, f32[8,128]{1,0:T(8,128)S(1)}, u32[]{:S(2)}, u32[]{:S(2)}) collective-permute-start(f32[8,128]{1,0:T(8,128)S(1)} %add.227), channel_id=1, source_target_pairs={{0,1},{1,0},{2,3},{3,2},{4,5},{5,4},{6,7},{7,6},{8,9},{9,8},{10,11... | collective-permute-start | bytes 12296 | tf_op jit(solution)/shard_map/ppermute | solution.py:196
  258.9 13.3 %collective-permute-done.57.refs_0_.refs_1_ = f32[8,2048]{1,0:T(8,128)S(1)} collective-permute-done((f32[8,2048]{1,0:T(8,128)S(1)}, f32[8,2048]{1,0:T(8,128)S(1)}, u32[]{:S(2)}, u32[]{:S(2)}) %collective-permute-start.57) | collective-permute-done | bytes 65568 | tf_op jit(solution)/shard_map/ppermute | solution.py:191
  276.8 4.1 collective-permute-start.61
  292.8 12.9 %collective-permute-done.66 = f32[8,128]{1,0:T(8,128)S(1)} collective-permute-done((f32[8,128]{1,0:T(8,128)S(1)}, f32[8,128]{1,0:T(8,128)S(1)}, u32[]{:S(2)}, u32[]{:S(2)}) %collective-permute-start.66) | collective-permute-done | bytes 4128 | tf_op jit(solution)/shard_map/ppermute | solution.py:191
  309.7 4.7 collective-permute-start.68
  325.9 12.9 %collective-permute-done.72 = f32[8,128]{1,0:T(8,128)S(1)} collective-permute-done((f32[8,128]{1,0:T(8,128)S(1)}, f32[8,128]{1,0:T(8,128)S(1)}, u32[]{:S(2)}, u32[]{:S(2)}) %collective-permute-start.72) | collective-permute-done | bytes 4128 | tf_op jit(solution)/shard_map/ppermute | solution.py:191
  340.1 2.7 collective-permute-done.73
  342.8 4.7 collective-permute-start.74
  359.2 12.7 %collective-permute-done.78 = f32[8,128]{1,0:T(8,128)S(1)} collective-permute-done((f32[8,128]{1,0:T(8,128)S(1)}, f32[8,128]{1,0:T(8,128)S(1)}, u32[]{:S(2)}, u32[]{:S(2)}) %collective-permute-start.78) | collective-permute-done | bytes 4128 | tf_op jit(solution)/shard_map/ppermute | solution.py:191
  373.2 2.7 collective-permute-done.79
  375.9 4.7 collective-permute-start.80
  392.1 12.9 %collective-permute-done.84 = f32[8,128]{1,0:T(8,128)S(1)} collective-permute-done((f32[8,128]{1,0:T(8,128)S(1)}, f32[8,128]{1,0:T(8,128)S(1)}, u32[]{:S(2)}, u32[]{:S(2)}) %collective-permute-start.84) | collective-permute-done | bytes 4128 | tf_op jit(solution)/shard_map/ppermute | solution.py:191
  406.2 2.7 collective-permute-done.85
  409.0 4.7 collective-permute-start.86
  425.2 12.9 %collective-permute-done.90 = f32[8,128]{1,0:T(8,128)S(1)} collective-permute-done((f32[8,128]{1,0:T(8,128)S(1)}, f32[8,128]{1,0:T(8,128)S(1)}, u32[]{:S(2)}, u32[]{:S(2)}) %collective-permute-start.90) | collective-permute-done | bytes 4128 | tf_op jit(solution)/shard_map/ppermute | solution.py:191
  439.3 2.8 collective-permute-done.91
  442.1 4.7 collective-permute-start.92
  458.3 12.9 %collective-permute-done.96 = f32[8,128]{1,0:T(8,128)S(1)} collective-permute-done((f32[8,128]{1,0:T(8,128)S(1)}, f32[8,128]{1,0:T(8,128)S(1)}, u32[]{:S(2)}, u32[]{:S(2)}) %collective-permute-start.96) | collective-permute-done | bytes 4128 | tf_op jit(solution)/shard_map/ppermute | solution.py:191
  472.6 2.8 collective-permute-done.97
  475.5 4.7 collective-permute-start.98
  491.7 12.9 %collective-permute-done.102 = f32[8,128]{1,0:T(8,128)S(1)} collective-permute-done((f32[8,128]{1,0:T(8,128)S(1)}, f32[8,128]{1,0:T(8,128)S(1)}, u32[]{:S(2)}, u32[]{:S(2)}) %collective-permute-start.102) | collective-permute-done | bytes 4128 | tf_op jit(solution)/shard_map/ppermute | solution.py:191
  505.7 2.9 collective-permute-done.103
  508.6 4.7 collective-permute-start.104
  522.6 12.9 %collective-permute-done.108 = f32[8,16384]{1,0:T(8,128)S(1)} collective-permute-done((f32[8,16384]{1,0:T(8,128)S(1)}, f32[8,16384]{1,0:T(8,128)S(1)}, u32[]{:S(2)}, u32[]{:S(2)}) %collective-permute-start.108) | collective-permute-done | bytes 524320 | tf_op jit(solution)/shard_map/ppermute | solution.py:191
  (321 shorter events, 243.6 us)
Async XLA Ops:
  33.8 16.4 %collective-permute-start.4 = (f32[8,16384]{1,0:T(8,128)S(1)}, f32[8,16384]{1,0:T(8,128)S(1)}, u32[]{:S(2)}, u32[]{:S(2)}) collective-permute-start(f32[8,16384]{1,0:T(8,128)S(1)} %update.16), channel_id=1, source_target_pairs={{0,16},{16,32},{32,48},{48,64},{64,80},{80,96},{96,112},{112,128},... | collective-permute-start | bytes 1572872 | tf_op jit(solution)/shard_map/ppermute | solution.py:191
  34.7 37.8 %collective-permute-start.10 = (f32[128,2048]{1,0:T(8,128)}, f32[128,2048]{1,0:T(8,128)S(1)}, u32[]{:S(2)}, u32[]{:S(2)}) collective-permute-start(f32[128,2048]{1,0:T(8,128)} %copy-done.17), channel_id=1, source_target_pairs={{0,240},{16,0},{32,16},{48,32},{64,48},{80,64},{96,80},{112,96},{1... | collective-permute-start | bytes 3145736 | tf_op jit(solution)/shard_map/ppermute | solution.py:191
  57.3 50.1 %collective-permute-start.18 = (f32[128,2048]{1,0:T(8,128)S(1)}, f32[128,2048]{1,0:T(8,128)S(1)}, u32[]{:S(2)}, u32[]{:S(2)}) collective-permute-start(f32[128,2048]{1,0:T(8,128)S(1)} %copy-done.16), channel_id=1, source_target_pairs={{0,240},{16,0},{32,16},{48,32},{64,48},{80,64},{96,80},{112,96},{1... | collective-permute-start | bytes 3145736 | tf_op jit(solution)/shard_map/ppermute | solution.py:191
  72.5 11.9 %collective-permute-start.9 = (f32[8,14336]{1,0:T(8,128)S(1)}, f32[8,14336]{1,0:T(8,128)S(1)}, u32[]{:S(2)}, u32[]{:S(2)}) collective-permute-start(f32[8,14336]{1,0:T(8,128)S(1)} %get-tuple-element.85), channel_id=1, source_target_pairs={{0,16},{16,32},{32,48},{48,64},{64,80},{80,96},{96,112},{112,128},... | collective-permute-start | bytes 1376264 | tf_op jit(solution)/shard_map/ppermute | solution.py:191
  73.2 11.3 %collective-permute-start.11 = (f32[8,128]{1,0:T(8,128)S(1)}, f32[8,128]{1,0:T(8,128)S(1)}, u32[]{:S(2)}, u32[]{:S(2)}) collective-permute-start(f32[8,128]{1,0:T(8,128)S(1)} %product.25), channel_id=1, source_target_pairs={{0,16},{16,32},{32,48},{48,64},{64,80},{80,96},{96,112},{112,128},... | collective-permute-start | bytes 12296 | tf_op jit(solution)/shard_map/ppermute | solution.py:191
  89.8 15.6 %collective-permute-start.16 = (f32[8,2048]{1,0:T(8,128)S(1)}, f32[8,2048]{1,0:T(8,128)S(1)}, u32[]{:S(2)}, u32[]{:S(2)}) collective-permute-start(f32[8,2048]{1,0:T(8,128)S(1)} %get-tuple-element.92.refs_0_), channel_id=1, source_target_pairs={{0,16},{16,32},{32,48},{48,64},{64,80},{80,96},{96,112},{112,128},... | collective-permute-start | bytes 196616 | tf_op jit(solution)/shard_map/ppermute | solution.py:191
  91.3 49.1 %collective-permute-start.26 = (f32[128,2048]{1,0:T(8,128)S(1)}, f32[128,2048]{1,0:T(8,128)S(1)}, u32[]{:S(2)}, u32[]{:S(2)}) collective-permute-start(f32[128,2048]{1,0:T(8,128)S(1)} %copy-done.14), channel_id=1, source_target_pairs={{0,240},{16,0},{32,16},{48,32},{64,48},{80,64},{96,80},{112,96},{1... | collective-permute-start | bytes 3145736 | tf_op jit(solution)/shard_map/ppermute | solution.py:191
  107.3 10.5 %collective-permute-start.17 = (f32[8,12288]{1,0:T(8,128)S(1)}, f32[8,12288]{1,0:T(8,128)S(1)}, u32[]{:S(2)}, u32[]{:S(2)}) collective-permute-start(f32[8,12288]{1,0:T(8,128)S(1)} %get-tuple-element.93), channel_id=1, source_target_pairs={{0,16},{16,32},{32,48},{48,64},{64,80},{80,96},{96,112},{112,128},... | collective-permute-start | bytes 1179656 | tf_op jit(solution)/shard_map/ppermute | solution.py:191
  108.3 9.6 %collective-permute-start.19 = (f32[8,128]{1,0:T(8,128)S(1)}, f32[8,128]{1,0:T(8,128)S(1)}, u32[]{:S(2)}, u32[]{:S(2)}) collective-permute-start(f32[8,128]{1,0:T(8,128)S(1)} %product.27), channel_id=1, source_target_pairs={{0,16},{16,32},{32,48},{48,64},{64,80},{80,96},{96,112},{112,128},... | collective-permute-start | bytes 12296 | tf_op jit(solution)/shard_map/ppermute | solution.py:191
  124.3 47.5 %collective-permute-start.34 = (f32[128,2048]{1,0:T(8,128)S(1)}, f32[128,2048]{1,0:T(8,128)S(1)}, u32[]{:S(2)}, u32[]{:S(2)}) collective-permute-start(f32[128,2048]{1,0:T(8,128)S(1)} %copy-done.12), channel_id=1, source_target_pairs={{0,240},{16,0},{32,16},{48,32},{64,48},{80,64},{96,80},{112,96},{1... | collective-permute-start | bytes 3145736 | tf_op jit(solution)/shard_map/ppermute | solution.py:191
  124.3 13.9 %collective-permute-start.24 = (f32[8,4096]{1,0:T(8,128)S(1)}, f32[8,4096]{1,0:T(8,128)S(1)}, u32[]{:S(2)}, u32[]{:S(2)}) collective-permute-start(f32[8,4096]{1,0:T(8,128)S(1)} %get-tuple-element.100.refs_0_), channel_id=1, source_target_pairs={{0,16},{16,32},{32,48},{48,64},{64,80},{80,96},{96,112},{112,128},... | collective-permute-start | bytes 393224 | tf_op jit(solution)/shard_map/ppermute | solution.py:191
  125.8 5.7 %collective-permute-start.21 = (f32[8,128]{1,0:T(8,128)S(1)}, f32[8,128]{1,0:T(8,128)S(1)}, u32[]{:S(2)}, u32[]{:S(2)}) collective-permute-start(f32[8,128]{1,0:T(8,128)S(1)} %add.211), channel_id=1, source_target_pairs={{0,1},{1,0},{2,3},{3,2},{4,5},{5,4},{6,7},{7,6},{8,9},{9,8},{10,11... | collective-permute-start | bytes 12296 | tf_op jit(solution)/shard_map/ppermute | solution.py:196
  140.2 9.1 %collective-permute-start.25 = (f32[8,10240]{1,0:T(8,128)S(1)}, f32[8,10240]{1,0:T(8,128)S(1)}, u32[]{:S(2)}, u32[]{:S(2)}) collective-permute-start(f32[8,10240]{1,0:T(8,128)S(1)} %get-tuple-element.101), channel_id=1, source_target_pairs={{0,16},{16,32},{32,48},{48,64},{64,80},{80,96},{96,112},{112,128},... | collective-permute-start | bytes 983048 | tf_op jit(solution)/shard_map/ppermute | solution.py:191
  141.5 8.0 %collective-permute-start.27 = (f32[8,128]{1,0:T(8,128)S(1)}, f32[8,128]{1,0:T(8,128)S(1)}, u32[]{:S(2)}, u32[]{:S(2)}) collective-permute-start(f32[8,128]{1,0:T(8,128)S(1)} %product.29), channel_id=1, source_target_pairs={{0,16},{16,32},{32,48},{48,64},{64,80},{80,96},{96,112},{112,128},... | collective-permute-start | bytes 12296 | tf_op jit(solution)/shard_map/ppermute | solution.py:191
  152.2 15.8 %collective-permute-start.32 = (f32[8,6144]{1,0:T(8,128)S(1)}, f32[8,6144]{1,0:T(8,128)S(1)}, u32[]{:S(2)}, u32[]{:S(2)}) collective-permute-start(f32[8,6144]{1,0:T(8,128)S(1)} %get-tuple-element.108.refs_0_), channel_id=1, source_target_pairs={{0,16},{16,32},{32,48},{48,64},{64,80},{80,96},{96,112},{112,128},... | collective-permute-start | bytes 589832 | tf_op jit(solution)/shard_map/ppermute | solution.py:191
  155.5 44.6 %collective-permute-start.42 = (f32[128,2048]{1,0:T(8,128)S(1)}, f32[128,2048]{1,0:T(8,128)S(1)}, u32[]{:S(2)}, u32[]{:S(2)}) collective-permute-start(f32[128,2048]{1,0:T(8,128)S(1)} %copy-done.10), channel_id=1, source_target_pairs={{0,240},{16,0},{32,16},{48,32},{64,48},{80,64},{96,80},{112,96},{1... | collective-permute-start | bytes 3145736 | tf_op jit(solution)/shard_map/ppermute | solution.py:191
  170.1 7.4 %collective-permute-start.33 = (f32[8,8192]{1,0:T(8,128)S(1)}, f32[8,8192]{1,0:T(8,128)S(1)}, u32[]{:S(2)}, u32[]{:S(2)}) collective-permute-start(f32[8,8192]{1,0:T(8,128)S(1)} %get-tuple-element.109), channel_id=1, source_target_pairs={{0,16},{16,32},{32,48},{48,64},{64,80},{80,96},{96,112},{112,128},... | collective-permute-start | bytes 786440 | tf_op jit(solution)/shard_map/ppermute | solution.py:191
  183.8 44.6 %collective-permute-start.50 = (f32[128,2048]{1,0:T(8,128)S(1)}, f32[128,2048]{1,0:T(8,128)S(1)}, u32[]{:S(2)}, u32[]{:S(2)}) collective-permute-start(f32[128,2048]{1,0:T(8,128)S(1)} %copy-done.8), channel_id=1, source_target_pairs={{0,240},{16,0},{32,16},{48,32},{64,48},{80,64},{96,80},{112,96},{1... | collective-permute-start | bytes 3145736 | tf_op jit(solution)/shard_map/ppermute | solution.py:191
  183.8 14.1 %collective-permute-start.40 = (f32[8,8192]{1,0:T(8,128)S(1)}, f32[8,8192]{1,0:T(8,128)S(1)}, u32[]{:S(2)}, u32[]{:S(2)}) collective-permute-start(f32[8,8192]{1,0:T(8,128)S(1)} %get-tuple-element.116.refs_0_), channel_id=1, source_target_pairs={{0,16},{16,32},{32,48},{48,64},{64,80},{80,96},{96,112},{112,128},... | collective-permute-start | bytes 786440 | tf_op jit(solution)/shard_map/ppermute | solution.py:191
  185.2 6.0 %collective-permute-start.37 = (f32[8,128]{1,0:T(8,128)S(1)}, f32[8,128]{1,0:T(8,128)S(1)}, u32[]{:S(2)}, u32[]{:S(2)}) collective-permute-start(f32[8,128]{1,0:T(8,128)S(1)} %add.219), channel_id=1, source_target_pairs={{0,1},{1,0},{2,3},{3,2},{4,5},{5,4},{6,7},{7,6},{8,9},{9,8},{10,11... | collective-permute-start | bytes 12296 | tf_op jit(solution)/shard_map/ppermute | solution.py:196
  200.0 6.7 %collective-permute-start.41 = (f32[8,6144]{1,0:T(8,128)S(1)}, f32[8,6144]{1,0:T(8,128)S(1)}, u32[]{:S(2)}, u32[]{:S(2)}) collective-permute-start(f32[8,6144]{1,0:T(8,128)S(1)} %get-tuple-element.117), channel_id=1, source_target_pairs={{0,16},{16,32},{32,48},{48,64},{64,80},{80,96},{96,112},{112,128},... | collective-permute-start | bytes 589832 | tf_op jit(solution)/shard_map/ppermute | solution.py:191
  209.3 16.4 %collective-permute-start.48 = (f32[8,10240]{1,0:T(8,128)S(1)}, f32[8,10240]{1,0:T(8,128)S(1)}, u32[]{:S(2)}, u32[]{:S(2)}) collective-permute-start(f32[8,10240]{1,0:T(8,128)S(1)} %get-tuple-element.124.refs_0_), channel_id=1, source_target_pairs={{0,16},{16,32},{32,48},{48,64},{64,80},{80,96},{96,112},{112,128},... | collective-permute-start | bytes 983048 | tf_op jit(solution)/shard_map/ppermute | solution.py:191
  211.9 44.5 %collective-permute-start.58 = (f32[128,2048]{1,0:T(8,128)S(1)}, f32[128,2048]{1,0:T(8,128)S(1)}, u32[]{:S(2)}, u32[]{:S(2)}) collective-permute-start(f32[128,2048]{1,0:T(8,128)S(1)} %get-tuple-element.135), channel_id=1, source_target_pairs={{0,240},{16,0},{32,16},{48,32},{64,48},{80,64},{96,80},{112,96},{1... | collective-permute-start | bytes 3145736 | tf_op jit(solution)/shard_map/ppermute | solution.py:191
  213.3 5.7 %collective-permute-start.45 = (f32[8,128]{1,0:T(8,128)S(1)}, f32[8,128]{1,0:T(8,128)S(1)}, u32[]{:S(2)}, u32[]{:S(2)}) collective-permute-start(f32[8,128]{1,0:T(8,128)S(1)} %add.223), channel_id=1, source_target_pairs={{0,1},{1,0},{2,3},{3,2},{4,5},{5,4},{6,7},{7,6},{8,9},{9,8},{10,11... | collective-permute-start | bytes 12296 | tf_op jit(solution)/shard_map/ppermute | solution.py:196
  227.8 6.0 %collective-permute-start.49 = (f32[8,4096]{1,0:T(8,128)S(1)}, f32[8,4096]{1,0:T(8,128)S(1)}, u32[]{:S(2)}, u32[]{:S(2)}) collective-permute-start(f32[8,4096]{1,0:T(8,128)S(1)} %get-tuple-element.125), channel_id=1, source_target_pairs={{0,16},{16,32},{32,48},{48,64},{64,80},{80,96},{96,112},{112,128},... | collective-permute-start | bytes 393224 | tf_op jit(solution)/shard_map/ppermute | solution.py:191
  239.7 50.4 %collective-permute-start.65 = (f32[128,2048]{1,0:T(8,128)S(1)}, f32[128,2048]{1,0:T(8,128)S(1)}, u32[]{:S(2)}, u32[]{:S(2)}) collective-permute-start(f32[128,2048]{1,0:T(8,128)S(1)} %get-tuple-element.139), channel_id=1, source_target_pairs={{0,240},{16,0},{32,16},{48,32},{64,48},{80,64},{96,80},{112,96},{1... | collective-permute-start | bytes 3145736 | tf_op jit(solution)/shard_map/ppermute | solution.py:191
  241.0 13.6 %collective-permute-start.56 = (f32[8,12288]{1,0:T(8,128)S(1)}, f32[8,12288]{1,0:T(8,128)S(1)}, u32[]{:S(2)}, u32[]{:S(2)}) collective-permute-start(f32[8,12288]{1,0:T(8,128)S(1)} %get-tuple-element.132.refs_0_), channel_id=1, source_target_pairs={{0,16},{16,32},{32,48},{48,64},{64,80},{80,96},{96,112},{112,128},... | collective-permute-start | bytes 1179656 | tf_op jit(solution)/shard_map/ppermute | solution.py:191
  241.2 6.3 %collective-permute-start.53 = (f32[8,128]{1,0:T(8,128)S(1)}, f32[8,128]{1,0:T(8,128)S(1)}, u32[]{:S(2)}, u32[]{:S(2)}) collective-permute-start(f32[8,128]{1,0:T(8,128)S(1)} %add.227), channel_id=1, source_target_pairs={{0,1},{1,0},{2,3},{3,2},{4,5},{5,4},{6,7},{7,6},{8,9},{9,8},{10,11... | collective-permute-start | bytes 12296 | tf_op jit(solution)/shard_map/ppermute | solution.py:196
  258.6 29.5 %collective-permute-start.64 = (f32[8,14336]{1,0:T(8,128)S(1)}, f32[8,14336]{1,0:T(8,128)S(1)}, u32[]{:S(2)}, u32[]{:S(2)}) collective-permute-start(f32[8,14336]{1,0:T(8,128)S(1)} %get-tuple-element.138.refs_0_), channel_id=1, source_target_pairs={{0,16},{16,32},{32,48},{48,64},{64,80},{80,96},{96,112},{112,128},... | collective-permute-start | bytes 1376264 | tf_op jit(solution)/shard_map/ppermute | solution.py:191
  258.7 13.5 %collective-permute-start.57 = (f32[8,2048]{1,0:T(8,128)S(1)}, f32[8,2048]{1,0:T(8,128)S(1)}, u32[]{:S(2)}, u32[]{:S(2)}) collective-permute-start(f32[8,2048]{1,0:T(8,128)S(1)} %get-tuple-element.133), channel_id=1, source_target_pairs={{0,16},{16,32},{32,48},{48,64},{64,80},{80,96},{96,112},{112,128},... | collective-permute-start | bytes 196616 | tf_op jit(solution)/shard_map/ppermute | solution.py:191
  258.8 13.5 %collective-permute-start.59 = (f32[8,128]{1,0:T(8,128)S(1)}, f32[8,128]{1,0:T(8,128)S(1)}, u32[]{:S(2)}, u32[]{:S(2)}) collective-permute-start(f32[8,128]{1,0:T(8,128)S(1)} %product.37), channel_id=1, source_target_pairs={{0,16},{16,32},{32,48},{48,64},{64,80},{80,96},{96,112},{112,128},... | collective-permute-start | bytes 12296 | tf_op jit(solution)/shard_map/ppermute | solution.py:191
  292.6 29.0 %collective-permute-start.71 = (f32[8,16384]{1,0:T(8,128)S(1)}, f32[8,16384]{1,0:T(8,128)S(1)}, u32[]{:S(2)}, u32[]{:S(2)}) collective-permute-start(f32[8,16384]{1,0:T(8,128)S(1)} %update.24.refs_0_), channel_id=1, source_target_pairs={{0,16},{16,32},{32,48},{48,64},{64,80},{80,96},{96,112},{112,128},... | collective-permute-start | bytes 1572872 | tf_op jit(solution)/shard_map/ppermute | solution.py:191
  292.7 13.0 %collective-permute-start.66 = (f32[8,128]{1,0:T(8,128)S(1)}, f32[8,128]{1,0:T(8,128)S(1)}, u32[]{:S(2)}, u32[]{:S(2)}) collective-permute-start(f32[8,128]{1,0:T(8,128)S(1)} %product.39), channel_id=1, source_target_pairs={{0,16},{16,32},{32,48},{48,64},{64,80},{80,96},{96,112},{112,128},... | collective-permute-start | bytes 12296 | tf_op jit(solution)/shard_map/ppermute | solution.py:191
  309.7 5.5 %collective-permute-start.68 = (f32[8,128]{1,0:T(8,128)S(1)}, f32[8,128]{1,0:T(8,128)S(1)}, u32[]{:S(2)}, u32[]{:S(2)}) collective-permute-start(f32[8,128]{1,0:T(8,128)S(1)} %add.235), channel_id=1, source_target_pairs={{0,1},{1,0},{2,3},{3,2},{4,5},{5,4},{6,7},{7,6},{8,9},{9,8},{10,11... | collective-permute-start | bytes 12296 | tf_op jit(solution)/shard_map/ppermute | solution.py:196
  325.7 29.0 %collective-permute-start.77 = (f32[8,16384]{1,0:T(8,128)S(1)}, f32[8,16384]{1,0:T(8,128)S(1)}, u32[]{:S(2)}, u32[]{:S(2)}) collective-permute-start(f32[8,16384]{1,0:T(8,128)S(1)} %update.25.refs_0_), channel_id=1, source_target_pairs={{0,16},{16,32},{32,48},{48,64},{64,80},{80,96},{96,112},{112,128},... | collective-permute-start | bytes 1572872 | tf_op jit(solution)/shard_map/ppermute | solution.py:191
  325.8 13.0 %collective-permute-start.72 = (f32[8,128]{1,0:T(8,128)S(1)}, f32[8,128]{1,0:T(8,128)S(1)}, u32[]{:S(2)}, u32[]{:S(2)}) collective-permute-start(f32[8,128]{1,0:T(8,128)S(1)} %product.40), channel_id=1, source_target_pairs={{0,16},{16,32},{32,48},{48,64},{64,80},{80,96},{96,112},{112,128},... | collective-permute-start | bytes 12296 | tf_op jit(solution)/shard_map/ppermute | solution.py:191
  342.8 5.5 %collective-permute-start.74 = (f32[8,128]{1,0:T(8,128)S(1)}, f32[8,128]{1,0:T(8,128)S(1)}, u32[]{:S(2)}, u32[]{:S(2)}) collective-permute-start(f32[8,128]{1,0:T(8,128)S(1)} %add.239), channel_id=1, source_target_pairs={{0,1},{1,0},{2,3},{3,2},{4,5},{5,4},{6,7},{7,6},{8,9},{9,8},{10,11... | collective-permute-start | bytes 12296 | tf_op jit(solution)/shard_map/ppermute | solution.py:196
  358.8 29.0 %collective-permute-start.83 = (f32[8,16384]{1,0:T(8,128)S(1)}, f32[8,16384]{1,0:T(8,128)S(1)}, u32[]{:S(2)}, u32[]{:S(2)}) collective-permute-start(f32[8,16384]{1,0:T(8,128)S(1)} %update.26.refs_0_), channel_id=1, source_target_pairs={{0,16},{16,32},{32,48},{48,64},{64,80},{80,96},{96,112},{112,128},... | collective-permute-start | bytes 1572872 | tf_op jit(solution)/shard_map/ppermute | solution.py:191
  358.9 13.0 %collective-permute-start.78 = (f32[8,128]{1,0:T(8,128)S(1)}, f32[8,128]{1,0:T(8,128)S(1)}, u32[]{:S(2)}, u32[]{:S(2)}) collective-permute-start(f32[8,128]{1,0:T(8,128)S(1)} %product.41), channel_id=1, source_target_pairs={{0,16},{16,32},{32,48},{48,64},{64,80},{80,96},{96,112},{112,128},... | collective-permute-start | bytes 12296 | tf_op jit(solution)/shard_map/ppermute | solution.py:191
  391.9 29.0 %collective-permute-start.89 = (f32[8,16384]{1,0:T(8,128)S(1)}, f32[8,16384]{1,0:T(8,128)S(1)}, u32[]{:S(2)}, u32[]{:S(2)}) collective-permute-start(f32[8,16384]{1,0:T(8,128)S(1)} %update.27.refs_0_), channel_id=1, source_target_pairs={{0,16},{16,32},{32,48},{48,64},{64,80},{80,96},{96,112},{112,128},... | collective-permute-start | bytes 1572872 | tf_op jit(solution)/shard_map/ppermute | solution.py:191
  392.0 13.0 %collective-permute-start.84 = (f32[8,128]{1,0:T(8,128)S(1)}, f32[8,128]{1,0:T(8,128)S(1)}, u32[]{:S(2)}, u32[]{:S(2)}) collective-permute-start(f32[8,128]{1,0:T(8,128)S(1)} %product.42), channel_id=1, source_target_pairs={{0,16},{16,32},{32,48},{48,64},{64,80},{80,96},{96,112},{112,128},... | collective-permute-start | bytes 12296 | tf_op jit(solution)/shard_map/ppermute | solution.py:191
  425.1 29.0 %collective-permute-start.95 = (f32[8,16384]{1,0:T(8,128)S(1)}, f32[8,16384]{1,0:T(8,128)S(1)}, u32[]{:S(2)}, u32[]{:S(2)}) collective-permute-start(f32[8,16384]{1,0:T(8,128)S(1)} %update.28.refs_0_), channel_id=1, source_target_pairs={{0,16},{16,32},{32,48},{48,64},{64,80},{80,96},{96,112},{112,128},... | collective-permute-start | bytes 1572872 | tf_op jit(solution)/shard_map/ppermute | solution.py:191
  425.1 13.0 %collective-permute-start.90 = (f32[8,128]{1,0:T(8,128)S(1)}, f32[8,128]{1,0:T(8,128)S(1)}, u32[]{:S(2)}, u32[]{:S(2)}) collective-permute-start(f32[8,128]{1,0:T(8,128)S(1)} %product.43), channel_id=1, source_target_pairs={{0,16},{16,32},{32,48},{48,64},{64,80},{80,96},{96,112},{112,128},... | collective-permute-start | bytes 12296 | tf_op jit(solution)/shard_map/ppermute | solution.py:191
  458.2 29.2 %collective-permute-start.101 = (f32[8,16384]{1,0:T(8,128)S(1)}, f32[8,16384]{1,0:T(8,128)S(1)}, u32[]{:S(2)}, u32[]{:S(2)}) collective-permute-start(f32[8,16384]{1,0:T(8,128)S(1)} %update.29.refs_0_), channel_id=1, source_target_pairs={{0,16},{16,32},{32,48},{48,64},{64,80},{80,96},{96,112},{112,128},... | collective-permute-start | bytes 1572872 | tf_op jit(solution)/shard_map/ppermute | solution.py:191
  458.2 13.0 %collective-permute-start.96 = (f32[8,128]{1,0:T(8,128)S(1)}, f32[8,128]{1,0:T(8,128)S(1)}, u32[]{:S(2)}, u32[]{:S(2)}) collective-permute-start(f32[8,128]{1,0:T(8,128)S(1)} %product.44), channel_id=1, source_target_pairs={{0,16},{16,32},{32,48},{48,64},{64,80},{80,96},{96,112},{112,128},... | collective-permute-start | bytes 12296 | tf_op jit(solution)/shard_map/ppermute | solution.py:191
  491.5 29.0 %collective-permute-start.107 = (f32[8,16384]{1,0:T(8,128)S(1)}, f32[8,16384]{1,0:T(8,128)S(1)}, u32[]{:S(2)}, u32[]{:S(2)}) collective-permute-start(f32[8,16384]{1,0:T(8,128)S(1)} %update.30.refs_0_), channel_id=1, source_target_pairs={{0,16},{16,32},{32,48},{48,64},{64,80},{80,96},{96,112},{112,128},... | collective-permute-start | bytes 1572872 | tf_op jit(solution)/shard_map/ppermute | solution.py:191
  491.6 13.0 %collective-permute-start.102 = (f32[8,128]{1,0:T(8,128)S(1)}, f32[8,128]{1,0:T(8,128)S(1)}, u32[]{:S(2)}, u32[]{:S(2)}) collective-permute-start(f32[8,128]{1,0:T(8,128)S(1)} %product.45), channel_id=1, source_target_pairs={{0,16},{16,32},{32,48},{48,64},{64,80},{80,96},{96,112},{112,128},... | collective-permute-start | bytes 12296 | tf_op jit(solution)/shard_map/ppermute | solution.py:191
  522.6 13.0 %collective-permute-start.108 = (f32[8,16384]{1,0:T(8,128)S(1)}, f32[8,16384]{1,0:T(8,128)S(1)}, u32[]{:S(2)}, u32[]{:S(2)}) collective-permute-start(f32[8,16384]{1,0:T(8,128)S(1)} %update.31), channel_id=1, source_target_pairs={{0,16},{16,32},{32,48},{48,64},{64,80},{80,96},{96,112},{112,128},... | collective-permute-start | bytes 1572872 | tf_op jit(solution)/shard_map/ppermute | solution.py:191
  (79 other events, 498.2 us)

commit v2 on v1

--- a/solution.py
+++ b/solution.py
@@ -65,21 +65,23 @@
     return own, copies
 
 
-def arrange_kernel(front_ref, meas_ref, o_ref):
-    for k in range(o_ref.shape[0]):
-        f = front_ref[k]
+def arrange_kernel(meas_ref, o_ref):
+    n = o_ref.shape[0]
+    position = lax.axis_index("rows")
+    for k in range(n):
+        f = lax.rem(position + (n - k), n)
         o_ref[k] = meas_ref[pl.ds(pl.multiple_of(f * 8, 8), 8), :]
 
 
-def arranged(measured, fronts):
-    n = fronts.shape[0]
+def arranged(measured, n):
     return pl.pallas_call(
         arrange_kernel,
-        in_specs=[SMEM, VMEM],
+        in_specs=[VMEM],
         out_specs=VMEM,
         out_shape=jax.ShapeDtypeStruct((n, measured.shape[0] // n, measured.shape[1]), f32),
+        compiler_params=pltpu.CompilerParams(vmem_limit_bytes=1 << 20),
         name="arranged",
-    )(fronts, measured)
+    )(measured)
 
 
 def turn_kernel(a_ref, *refs):
@@ -112,6 +114,10 @@
     return pl.ds(pl.multiple_of(c * CHUNK, CHUNK), CHUNK)
 
 
+def looped(low, high, step):
+    lax.fori_loop(low, high, step, 0, unroll=2 if (high - low) % 2 == 0 else 1)
+
+
 def product_kernel(first, turned, add, *refs):
     x_ref, a_ref = refs[0], refs[1]
     o_ref, acc = refs[-2], refs[-1]
@@ -127,7 +133,7 @@
             )
         return 0
 
-    lax.fori_loop(0, x_ref.shape[1] // CHUNK, step, 0)
+    looped(0, x_ref.shape[1] // CHUNK, step)
     both = acc[0:8, :] + acc[8:16, :]
     p = both[:, :128] + both[:, 128:]
     o_ref[...] = p + refs[2][...] if add else p
@@ -170,7 +176,7 @@
             o_ref[:, at(c - o0)] = jnp.clip(x, lower_bound, upper_bound)
             return 0
 
-        lax.fori_loop(low, high, step, 0)
+        looped(low, high, step)
 
 
 def update(k, total, wanted, a, pieces, ins, outs):
@@ -191,6 +197,12 @@
     return lax.ppermute(block, "rows", [(i, (i + distance) % n) for i in range(n)])
 
 
+def shifted_across(block, reach):
+    n, m = lax.axis_size("rows"), lax.axis_size("vox")
+    pairs = [(r * m + v, (r + 1) % n * m + (v ^ reach)) for r in range(n) for v in range(m)]
+    return lax.ppermute(block, ("rows", "vox"), pairs)
+
+
 def exchanged(p, reach):
     n = lax.axis_size("vox")
     return p + lax.ppermute(p, "vox", [(i, i ^ reach) for i in range(n)])
@@ -202,20 +214,19 @@
 
 def shards(system, measured, start_image):
     cycle = lax.axis_size("rows")
-    position = lax.axis_index("rows")
     n = system.shape[1] // CHUNK
-    fronts = ((position - jnp.arange(cycle)) % cycle).astype(jnp.int32)
-    wanted = arranged(measured, fronts)
+    wanted = arranged(measured, cycle)
     own, chunks = split_rows(system)
     arriving = []
     following = None
-    pieces, ins, held = [start_image], (n,), 0
+    pieces, ins, held, crossed = [start_image], (n,), 0, False
     p = product(start_image, own, 0, False, None)
     for k in range(cycle):
         last = k == cycle - 1
         now = 0 if last else HELD[k]
         outs = ends(now, n)
-        p = exchanged(p, 8)
+        if not crossed:
+            p = exchanged(p, 8)
         if len(arriving) < n and not last:
             p, chunk = barrier((p, chunks[len(arriving)]))
             arriving.append(shifted(chunk, -1))
@@ -236,7 +247,12 @@
         else:
             p = product(new[0], following, 0, True, None)
             p, kept = barrier((p, new[0]))
+            crossed = now == n
+            if crossed:
+                across = shifted_across(p, 8)
             p = shifted(p, 1)
+            if crossed:
+                p = p + across
             near = shifted(kept, 1)
             if now < n:
                 p = product(far, own, now, False, p)

time: 547 us -> 494 us (0.903)
  the two profiles are of different devices: /device:TPU:1 before, /device:TPU:8 now
where the time goes in v2:
time: 494 us; the launch traced here: 485 us
  waiting for transfers between devices  324 us (66%)
  starting transfers between devices  90.9 us (18%)
  Pallas kernels  64.3 us (13%)
    ppermute x45, waiting for transfers between devices, shifted(): lax.ppermute(block, 'rows', [(i, (i + distance) % n) for i in range(n)])  181 us
    ppermute x57, waiting for transfers between devices, exchanged(): return p + lax.ppermute(p, 'vox', [(i, i ^ reach) for i in range(n)])  141 us
    ppermute x57, starting transfers between devices, exchanged(): return p + lax.ppermute(p, 'vox', [(i, i ^ reach) for i in range(n)])  64.6 us
    pallas_call x23, Pallas kernels, product(): pl.pallas_call(functools.partial(product_kernel, first, turned, before is...  33 us
    pallas_call x16, Pallas kernels, update(): pl.pallas_call(functools.partial(update_kernel, k, ins, outs), in_specs=[...  26.7 us
    ppermute x45, starting transfers between devices, shifted(): lax.ppermute(block, 'rows', [(i, (i + distance) % n) for i in range(n)])  23.9 us
  transfers between devices with their start and end apart: 109, of which 83 were waited for; matrix products, arithmetic and copies ran while one was open for 0% of the time, Pallas kernels for 7%

profile of v2, /device:TPU:8, one launch (start us, length us, event | category | flops | bytes accessed | tf_op | source)
XLA Modules:
  0.0 485.0 jit_solution(3598651443538781417)
XLA Ops:
  0.0 3.4 copy-done
  7.8 3.1 collective-permute-start
  20.1 2.9 collective-permute-done.3
  26.4 5.0 %collective-permute-start.10 = (f32[128,2048]{1,0:T(8,128)S(1)}, f32[128,2048]{1,0:T(8,128)S(1)}, u32[]{:S(2)}, u32[]{:S(2)}) collective-permute-start(f32[128,2048]{1,0:T(8,128)S(1)} %get-tuple-element.87), channel_id=1, source_target_pairs={{0,240},{16,0},{32,16},{48,32},{64,48},{80,64},{96,80},{112,96},{1... | collective-permute-start | bytes 3145736 | tf_op jit(solution)/shard_map/ppermute | solution.py:197
  31.4 9.9 %collective-permute-done.4.refs_0_ = f32[8,16384]{1,0:T(8,128)S(1)} collective-permute-done((f32[8,16384]{1,0:T(8,128)S(1)}, f32[8,16384]{1,0:T(8,128)S(1)}, u32[]{:S(2)}, u32[]{:S(2)}) %collective-permute-start.4) | collective-permute-done | bytes 524320 | tf_op jit(solution)/shard_map/ppermute | solution.py:197
  52.8 3.2 collective-permute-done.7
  63.8 12.1 %collective-permute-done.9.refs_0_.refs_1_ = f32[8,14336]{1,0:T(8,128)S(1)} collective-permute-done((f32[8,14336]{1,0:T(8,128)S(1)}, f32[8,14336]{1,0:T(8,128)S(1)}, u32[]{:S(2)}, u32[]{:S(2)}) %collective-permute-start.9) | collective-permute-done | bytes 458784 | tf_op jit(solution)/shard_map/ppermute | solution.py:197
  87.6 3.2 collective-permute-done.14
  98.5 10.3 %collective-permute-done.17.refs_0_.refs_1_ = f32[8,12288]{1,0:T(8,128)S(1)} collective-permute-done((f32[8,12288]{1,0:T(8,128)S(1)}, f32[8,12288]{1,0:T(8,128)S(1)}, u32[]{:S(2)}, u32[]{:S(2)}) %collective-permute-start.17) | collective-permute-done | bytes 393248 | tf_op jit(solution)/shard_map/ppermute | solution.py:197
  112.0 4.1 collective-permute-done.20
  119.7 3.2 collective-permute-done.22
  131.1 8.7 %collective-permute-done.25.refs_0_.refs_1_ = f32[8,10240]{1,0:T(8,128)S(1)} collective-permute-done((f32[8,10240]{1,0:T(8,128)S(1)}, f32[8,10240]{1,0:T(8,128)S(1)}, u32[]{:S(2)}, u32[]{:S(2)}) %collective-permute-start.25) | collective-permute-done | bytes 327712 | tf_op jit(solution)/shard_map/ppermute | solution.py:197
  143.1 4.3 collective-permute-done.28
  149.0 3.2 collective-permute-done.30
  162.4 5.3 %collective-permute-done.33.refs_0_.refs_1_ = f32[8,8192]{1,0:T(8,128)S(1)} collective-permute-done((f32[8,8192]{1,0:T(8,128)S(1)}, f32[8,8192]{1,0:T(8,128)S(1)}, u32[]{:S(2)}, u32[]{:S(2)}) %collective-permute-start.33) | collective-permute-done | bytes 262176 | tf_op jit(solution)/shard_map/ppermute | solution.py:197
  171.4 3.1 collective-permute-done.36
  178.2 3.2 collective-permute-done.38
  190.5 5.6 %collective-permute-done.41.refs_0_.refs_1_ = f32[8,6144]{1,0:T(8,128)S(1)} collective-permute-done((f32[8,6144]{1,0:T(8,128)S(1)}, f32[8,6144]{1,0:T(8,128)S(1)}, u32[]{:S(2)}, u32[]{:S(2)}) %collective-permute-start.41) | collective-permute-done | bytes 196640 | tf_op jit(solution)/shard_map/ppermute | solution.py:197
  199.5 3.5 collective-permute-done.44
  206.2 3.2 collective-permute-done.46
  218.4 5.1 %collective-permute-done.49.refs_0_.refs_1_ = f32[8,4096]{1,0:T(8,128)S(1)} collective-permute-done((f32[8,4096]{1,0:T(8,128)S(1)}, f32[8,4096]{1,0:T(8,128)S(1)}, u32[]{:S(2)}, u32[]{:S(2)}) %collective-permute-start.49) | collective-permute-done | bytes 131104 | tf_op jit(solution)/shard_map/ppermute | solution.py:197
  226.7 3.1 collective-permute-done.52
  233.5 3.2 collective-permute-done.54
  245.9 14.2 %collective-permute-done.57.refs_0_.refs_1_ = f32[8,2048]{1,0:T(8,128)S(1)} collective-permute-done((f32[8,2048]{1,0:T(8,128)S(1)}, f32[8,2048]{1,0:T(8,128)S(1)}, u32[]{:S(2)}, u32[]{:S(2)}) %collective-permute-start.57) | collective-permute-done | bytes 65568 | tf_op jit(solution)/shard_map/ppermute | solution.py:197
  262.6 3.1 collective-permute-done.60
  267.3 3.2 collective-permute-done.62
  279.8 13.7 %collective-permute-done.66 = f32[8,128]{1,0:T(8,128)S(1)} collective-permute-done((f32[8,128]{1,0:T(8,128)S(1)}, f32[8,128]{1,0:T(8,128)S(1)}, u32[]{:S(2)}, u32[]{:S(2)}) %collective-permute-start.66) | collective-permute-done | bytes 4128 | tf_op jit(solution)/shard_map/ppermute | solution.py:197
  295.7 3.2 collective-permute-done.69
  301.2 2.8 collective-permute-done.70
  307.4 13.7 %collective-permute-done.72 = f32[8,128]{1,0:T(8,128)S(1)} collective-permute-done((f32[8,128]{1,0:T(8,128)S(1)}, f32[8,128]{1,0:T(8,128)S(1)}, u32[]{:S(2)}, u32[]{:S(2)}) %collective-permute-start.72) | collective-permute-done | bytes 4128 | tf_op jit(solution)/shard_map/ppermute | solution.py:197
  323.0 3.2 collective-permute-done.75
  328.5 2.8 collective-permute-done.76
  335.2 13.3 %collective-permute-done.78 = f32[8,128]{1,0:T(8,128)S(1)} collective-permute-done((f32[8,128]{1,0:T(8,128)S(1)}, f32[8,128]{1,0:T(8,128)S(1)}, u32[]{:S(2)}, u32[]{:S(2)}) %collective-permute-start.78) | collective-permute-done | bytes 4128 | tf_op jit(solution)/shard_map/ppermute | solution.py:197
  350.6 3.2 collective-permute-done.81
  356.1 2.8 collective-permute-done.82
  362.3 13.7 %collective-permute-done.84 = f32[8,128]{1,0:T(8,128)S(1)} collective-permute-done((f32[8,128]{1,0:T(8,128)S(1)}, f32[8,128]{1,0:T(8,128)S(1)}, u32[]{:S(2)}, u32[]{:S(2)}) %collective-permute-start.84) | collective-permute-done | bytes 4128 | tf_op jit(solution)/shard_map/ppermute | solution.py:197
  377.8 3.2 collective-permute-done.87
  383.2 2.8 collective-permute-done.88
  390.1 13.0 %collective-permute-done.90 = f32[8,128]{1,0:T(8,128)S(1)} collective-permute-done((f32[8,128]{1,0:T(8,128)S(1)}, f32[8,128]{1,0:T(8,128)S(1)}, u32[]{:S(2)}, u32[]{:S(2)}) %collective-permute-start.90) | collective-permute-done | bytes 4128 | tf_op jit(solution)/shard_map/ppermute | solution.py:197
  405.3 3.2 collective-permute-done.93
  410.8 2.8 collective-permute-done.94
  417.0 13.7 %collective-permute-done.96 = f32[8,128]{1,0:T(8,128)S(1)} collective-permute-done((f32[8,128]{1,0:T(8,128)S(1)}, f32[8,128]{1,0:T(8,128)S(1)}, u32[]{:S(2)}, u32[]{:S(2)}) %collective-permute-start.96) | collective-permute-done | bytes 4128 | tf_op jit(solution)/shard_map/ppermute | solution.py:197
  432.5 3.2 collective-permute-done.99
  437.9 2.8 collective-permute-done.100
  444.6 13.3 %collective-permute-done.102 = f32[8,128]{1,0:T(8,128)S(1)} collective-permute-done((f32[8,128]{1,0:T(8,128)S(1)}, f32[8,128]{1,0:T(8,128)S(1)}, u32[]{:S(2)}, u32[]{:S(2)}) %collective-permute-start.102) | collective-permute-done | bytes 4128 | tf_op jit(solution)/shard_map/ppermute | solution.py:197
  460.0 3.2 collective-permute-done.105
  465.5 2.8 collective-permute-done.106
  470.0 13.8 %collective-permute-done.108 = f32[8,16384]{1,0:T(8,128)S(1)} collective-permute-done((f32[8,16384]{1,0:T(8,128)S(1)}, f32[8,16384]{1,0:T(8,128)S(1)}, u32[]{:S(2)}, u32[]{:S(2)}) %collective-permute-start.108) | collective-permute-done | bytes 524320 | tf_op jit(solution)/shard_map/ppermute | solution.py:197
  (290 shorter events, 201.8 us)
Async XLA Ops:
  24.6 16.7 %collective-permute-start.4 = (f32[8,16384]{1,0:T(8,128)S(1)}, f32[8,16384]{1,0:T(8,128)S(1)}, u32[]{:S(2)}, u32[]{:S(2)}) collective-permute-start(f32[8,16384]{1,0:T(8,128)S(1)} %update.16), channel_id=1, source_target_pairs={{0,16},{16,32},{32,48},{48,64},{64,80},{80,96},{96,112},{112,128},... | collective-permute-start | bytes 1572872 | tf_op jit(solution)/shard_map/ppermute | solution.py:197
  26.4 36.7 %collective-permute-start.10 = (f32[128,2048]{1,0:T(8,128)S(1)}, f32[128,2048]{1,0:T(8,128)S(1)}, u32[]{:S(2)}, u32[]{:S(2)}) collective-permute-start(f32[128,2048]{1,0:T(8,128)S(1)} %get-tuple-element.87), channel_id=1, source_target_pairs={{0,240},{16,0},{32,16},{48,32},{64,48},{80,64},{96,80},{112,96},{1... | collective-permute-start | bytes 3145736 | tf_op jit(solution)/shard_map/ppermute | solution.py:197
  49.1 48.7 %collective-permute-start.18 = (f32[128,2048]{1,0:T(8,128)S(1)}, f32[128,2048]{1,0:T(8,128)S(1)}, u32[]{:S(2)}, u32[]{:S(2)}) collective-permute-start(f32[128,2048]{1,0:T(8,128)S(1)} %get-tuple-element.95), channel_id=1, source_target_pairs={{0,240},{16,0},{32,16},{48,32},{64,48},{80,64},{96,80},{112,96},{1... | collective-permute-start | bytes 3145736 | tf_op jit(solution)/shard_map/ppermute | solution.py:197
  63.1 12.8 %collective-permute-start.9 = (f32[8,14336]{1,0:T(8,128)S(1)}, f32[8,14336]{1,0:T(8,128)S(1)}, u32[]{:S(2)}, u32[]{:S(2)}) collective-permute-start(f32[8,14336]{1,0:T(8,128)S(1)} %get-tuple-element.85), channel_id=1, source_target_pairs={{0,16},{16,32},{32,48},{48,64},{64,80},{80,96},{96,112},{112,128},... | collective-permute-start | bytes 1376264 | tf_op jit(solution)/shard_map/ppermute | solution.py:197
  63.8 12.2 %collective-permute-start.11 = (f32[8,128]{1,0:T(8,128)S(1)}, f32[8,128]{1,0:T(8,128)S(1)}, u32[]{:S(2)}, u32[]{:S(2)}) collective-permute-start(f32[8,128]{1,0:T(8,128)S(1)} %product.25), channel_id=1, source_target_pairs={{0,16},{16,32},{32,48},{48,64},{64,80},{80,96},{96,112},{112,128},... | collective-permute-start | bytes 12296 | tf_op jit(solution)/shard_map/ppermute | solution.py:197
  81.5 14.4 %collective-permute-start.16 = (f32[8,2048]{1,0:T(8,128)S(1)}, f32[8,2048]{1,0:T(8,128)S(1)}, u32[]{:S(2)}, u32[]{:S(2)}) collective-permute-start(f32[8,2048]{1,0:T(8,128)S(1)} %get-tuple-element.92.refs_0_), channel_id=1, source_target_pairs={{0,16},{16,32},{32,48},{48,64},{64,80},{80,96},{96,112},{112,128},... | collective-permute-start | bytes 196616 | tf_op jit(solution)/shard_map/ppermute | solution.py:197
  83.9 46.0 %collective-permute-start.26 = (f32[128,2048]{1,0:T(8,128)S(1)}, f32[128,2048]{1,0:T(8,128)S(1)}, u32[]{:S(2)}, u32[]{:S(2)}) collective-permute-start(f32[128,2048]{1,0:T(8,128)S(1)} %get-tuple-element.103), channel_id=1, source_target_pairs={{0,240},{16,0},{32,16},{48,32},{64,48},{80,64},{96,80},{112,96},{1... | collective-permute-start | bytes 3145736 | tf_op jit(solution)/shard_map/ppermute | solution.py:197
  97.5 11.4 %collective-permute-start.17 = (f32[8,12288]{1,0:T(8,128)S(1)}, f32[8,12288]{1,0:T(8,128)S(1)}, u32[]{:S(2)}, u32[]{:S(2)}) collective-permute-start(f32[8,12288]{1,0:T(8,128)S(1)} %get-tuple-element.93), channel_id=1, source_target_pairs={{0,16},{16,32},{32,48},{48,64},{64,80},{80,96},{96,112},{112,128},... | collective-permute-start | bytes 1179656 | tf_op jit(solution)/shard_map/ppermute | solution.py:197
  98.5 10.4 %collective-permute-start.19 = (f32[8,128]{1,0:T(8,128)S(1)}, f32[8,128]{1,0:T(8,128)S(1)}, u32[]{:S(2)}, u32[]{:S(2)}) collective-permute-start(f32[8,128]{1,0:T(8,128)S(1)} %product.27), channel_id=1, source_target_pairs={{0,16},{16,32},{32,48},{48,64},{64,80},{80,96},{96,112},{112,128},... | collective-permute-start | bytes 12296 | tf_op jit(solution)/shard_map/ppermute | solution.py:197
  116.1 45.1 %collective-permute-start.34 = (f32[128,2048]{1,0:T(8,128)S(1)}, f32[128,2048]{1,0:T(8,128)S(1)}, u32[]{:S(2)}, u32[]{:S(2)}) collective-permute-start(f32[128,2048]{1,0:T(8,128)S(1)} %get-tuple-element.111), channel_id=1, source_target_pairs={{0,240},{16,0},{32,16},{48,32},{64,48},{80,64},{96,80},{112,96},{1... | collective-permute-start | bytes 3145736 | tf_op jit(solution)/shard_map/ppermute | solution.py:197
  116.1 11.9 %collective-permute-start.24 = (f32[8,4096]{1,0:T(8,128)S(1)}, f32[8,4096]{1,0:T(8,128)S(1)}, u32[]{:S(2)}, u32[]{:S(2)}) collective-permute-start(f32[8,4096]{1,0:T(8,128)S(1)} %get-tuple-element.100.refs_0_), channel_id=1, source_target_pairs={{0,16},{16,32},{32,48},{48,64},{64,80},{80,96},{96,112},{112,128},... | collective-permute-start | bytes 393224 | tf_op jit(solution)/shard_map/ppermute | solution.py:197
  129.8 10.0 %collective-permute-start.25 = (f32[8,10240]{1,0:T(8,128)S(1)}, f32[8,10240]{1,0:T(8,128)S(1)}, u32[]{:S(2)}, u32[]{:S(2)}) collective-permute-start(f32[8,10240]{1,0:T(8,128)S(1)} %get-tuple-element.101), channel_id=1, source_target_pairs={{0,16},{16,32},{32,48},{48,64},{64,80},{80,96},{96,112},{112,128},... | collective-permute-start | bytes 983048 | tf_op jit(solution)/shard_map/ppermute | solution.py:197
  131.0 8.8 %collective-permute-start.27 = (f32[8,128]{1,0:T(8,128)S(1)}, f32[8,128]{1,0:T(8,128)S(1)}, u32[]{:S(2)}, u32[]{:S(2)}) collective-permute-start(f32[8,128]{1,0:T(8,128)S(1)} %product.29), channel_id=1, source_target_pairs={{0,16},{16,32},{32,48},{48,64},{64,80},{80,96},{96,112},{112,128},... | collective-permute-start | bytes 12296 | tf_op jit(solution)/shard_map/ppermute | solution.py:197
  142.9 14.4 %collective-permute-start.32 = (f32[8,6144]{1,0:T(8,128)S(1)}, f32[8,6144]{1,0:T(8,128)S(1)}, u32[]{:S(2)}, u32[]{:S(2)}) collective-permute-start(f32[8,6144]{1,0:T(8,128)S(1)} %get-tuple-element.108.refs_0_), channel_id=1, source_target_pairs={{0,16},{16,32},{32,48},{48,64},{64,80},{80,96},{96,112},{112,128},... | collective-permute-start | bytes 589832 | tf_op jit(solution)/shard_map/ppermute | solution.py:197
  147.4 41.0 %collective-permute-start.42 = (f32[128,2048]{1,0:T(8,128)S(1)}, f32[128,2048]{1,0:T(8,128)S(1)}, u32[]{:S(2)}, u32[]{:S(2)}) collective-permute-start(f32[128,2048]{1,0:T(8,128)S(1)} %get-tuple-element.119), channel_id=1, source_target_pairs={{0,240},{16,0},{32,16},{48,32},{64,48},{80,64},{96,80},{112,96},{1... | collective-permute-start | bytes 3145736 | tf_op jit(solution)/shard_map/ppermute | solution.py:197
  159.1 8.6 %collective-permute-start.33 = (f32[8,8192]{1,0:T(8,128)S(1)}, f32[8,8192]{1,0:T(8,128)S(1)}, u32[]{:S(2)}, u32[]{:S(2)}) collective-permute-start(f32[8,8192]{1,0:T(8,128)S(1)} %get-tuple-element.109), channel_id=1, source_target_pairs={{0,16},{16,32},{32,48},{48,64},{64,80},{80,96},{96,112},{112,128},... | collective-permute-start | bytes 786440 | tf_op jit(solution)/shard_map/ppermute | solution.py:197
  174.6 42.2 %collective-permute-start.50 = (f32[128,2048]{1,0:T(8,128)S(1)}, f32[128,2048]{1,0:T(8,128)S(1)}, u32[]{:S(2)}, u32[]{:S(2)}) collective-permute-start(f32[128,2048]{1,0:T(8,128)S(1)} %get-tuple-element.127), channel_id=1, source_target_pairs={{0,240},{16,0},{32,16},{48,32},{64,48},{80,64},{96,80},{112,96},{1... | collective-permute-start | bytes 3145736 | tf_op jit(solution)/shard_map/ppermute | solution.py:197
  174.6 11.9 %collective-permute-start.40 = (f32[8,8192]{1,0:T(8,128)S(1)}, f32[8,8192]{1,0:T(8,128)S(1)}, u32[]{:S(2)}, u32[]{:S(2)}) collective-permute-start(f32[8,8192]{1,0:T(8,128)S(1)} %get-tuple-element.116.refs_0_), channel_id=1, source_target_pairs={{0,16},{16,32},{32,48},{48,64},{64,80},{80,96},{96,112},{112,128},... | collective-permute-start | bytes 786440 | tf_op jit(solution)/shard_map/ppermute | solution.py:197
  188.3 7.9 %collective-permute-start.41 = (f32[8,6144]{1,0:T(8,128)S(1)}, f32[8,6144]{1,0:T(8,128)S(1)}, u32[]{:S(2)}, u32[]{:S(2)}) collective-permute-start(f32[8,6144]{1,0:T(8,128)S(1)} %get-tuple-element.117), channel_id=1, source_target_pairs={{0,16},{16,32},{32,48},{48,64},{64,80},{80,96},{96,112},{112,128},... | collective-permute-start | bytes 589832 | tf_op jit(solution)/shard_map/ppermute | solution.py:197
  199.5 15.0 %collective-permute-start.48 = (f32[8,10240]{1,0:T(8,128)S(1)}, f32[8,10240]{1,0:T(8,128)S(1)}, u32[]{:S(2)}, u32[]{:S(2)}) collective-permute-start(f32[8,10240]{1,0:T(8,128)S(1)} %get-tuple-element.124.refs_0_), channel_id=1, source_target_pairs={{0,16},{16,32},{32,48},{48,64},{64,80},{80,96},{96,112},{112,128},... | collective-permute-start | bytes 983048 | tf_op jit(solution)/shard_map/ppermute | solution.py:197
  203.0 40.3 %collective-permute-start.58 = (f32[128,2048]{1,0:T(8,128)S(1)}, f32[128,2048]{1,0:T(8,128)S(1)}, u32[]{:S(2)}, u32[]{:S(2)}) collective-permute-start(f32[128,2048]{1,0:T(8,128)S(1)} %get-tuple-element.135), channel_id=1, source_target_pairs={{0,240},{16,0},{32,16},{48,32},{64,48},{80,64},{96,80},{112,96},{1... | collective-permute-start | bytes 3145736 | tf_op jit(solution)/shard_map/ppermute | solution.py:197
  229.8 47.8 %collective-permute-start.65 = (f32[128,2048]{1,0:T(8,128)S(1)}, f32[128,2048]{1,0:T(8,128)S(1)}, u32[]{:S(2)}, u32[]{:S(2)}) collective-permute-start(f32[128,2048]{1,0:T(8,128)S(1)} %get-tuple-element.139), channel_id=1, source_target_pairs={{0,240},{16,0},{32,16},{48,32},{64,48},{80,64},{96,80},{112,96},{1... | collective-permute-start | bytes 3145736 | tf_op jit(solution)/shard_map/ppermute | solution.py:197
  231.4 10.3 %collective-permute-start.56 = (f32[8,12288]{1,0:T(8,128)S(1)}, f32[8,12288]{1,0:T(8,128)S(1)}, u32[]{:S(2)}, u32[]{:S(2)}) collective-permute-start(f32[8,12288]{1,0:T(8,128)S(1)} %get-tuple-element.132.refs_0_), channel_id=1, source_target_pairs={{0,16},{16,32},{32,48},{48,64},{64,80},{80,96},{96,112},{112,128},... | collective-permute-start | bytes 1179656 | tf_op jit(solution)/shard_map/ppermute | solution.py:197
  245.5 30.1 %collective-permute-start.64 = (f32[8,14336]{1,0:T(8,128)S(1)}, f32[8,14336]{1,0:T(8,128)S(1)}, u32[]{:S(2)}, u32[]{:S(2)}) collective-permute-start(f32[8,14336]{1,0:T(8,128)S(1)} %get-tuple-element.138.refs_0_), channel_id=1, source_target_pairs={{0,16},{16,32},{32,48},{48,64},{64,80},{80,96},{96,112},{112,128},... | collective-permute-start | bytes 1376264 | tf_op jit(solution)/shard_map/ppermute | solution.py:197
  245.7 14.4 %collective-permute-start.57 = (f32[8,2048]{1,0:T(8,128)S(1)}, f32[8,2048]{1,0:T(8,128)S(1)}, u32[]{:S(2)}, u32[]{:S(2)}) collective-permute-start(f32[8,2048]{1,0:T(8,128)S(1)} %get-tuple-element.133), channel_id=1, source_target_pairs={{0,16},{16,32},{32,48},{48,64},{64,80},{80,96},{96,112},{112,128},... | collective-permute-start | bytes 196616 | tf_op jit(solution)/shard_map/ppermute | solution.py:197
  245.8 14.4 %collective-permute-start.59 = (f32[8,128]{1,0:T(8,128)S(1)}, f32[8,128]{1,0:T(8,128)S(1)}, u32[]{:S(2)}, u32[]{:S(2)}) collective-permute-start(f32[8,128]{1,0:T(8,128)S(1)} %product.37), channel_id=1, source_target_pairs={{0,16},{16,32},{32,48},{48,64},{64,80},{80,96},{96,112},{112,128},... | collective-permute-start | bytes 12296 | tf_op jit(solution)/shard_map/ppermute | solution.py:197
  279.6 24.4 %collective-permute-start.71 = (f32[8,16384]{1,0:T(8,128)S(1)}, f32[8,16384]{1,0:T(8,128)S(1)}, u32[]{:S(2)}, u32[]{:S(2)}) collective-permute-start(f32[8,16384]{1,0:T(8,128)S(1)} %update.24.refs_0_), channel_id=1, source_target_pairs={{0,16},{16,32},{32,48},{48,64},{64,80},{80,96},{96,112},{112,128},... | collective-permute-start | bytes 1572872 | tf_op jit(solution)/shard_map/ppermute | solution.py:197
  279.6 13.9 %collective-permute-start.66 = (f32[8,128]{1,0:T(8,128)S(1)}, f32[8,128]{1,0:T(8,128)S(1)}, u32[]{:S(2)}, u32[]{:S(2)}) collective-permute-start(f32[8,128]{1,0:T(8,128)S(1)} %product.39), channel_id=1, source_target_pairs={{0,16},{16,32},{32,48},{48,64},{64,80},{80,96},{96,112},{112,128},... | collective-permute-start | bytes 12296 | tf_op jit(solution)/shard_map/ppermute | solution.py:197
  279.7 14.4 %collective-permute-start.67 = (f32[8,128]{1,0:T(8,128)S(1)}, f32[8,128]{1,0:T(8,128)S(1)}, u32[]{:S(2)}, u32[]{:S(2)}) collective-permute-start(f32[8,128]{1,0:T(8,128)S(1)} %product.39), channel_id=1, source_target_pairs={{0,24},{1,25},{2,26},{3,27},{4,28},{5,29},{6,30},{7,31},{8,16},{9,... | collective-permute-start | bytes 12296 | tf_op jit(solution)/shard_map/ppermute | solution.py:203
  307.1 24.2 %collective-permute-start.77 = (f32[8,16384]{1,0:T(8,128)S(1)}, f32[8,16384]{1,0:T(8,128)S(1)}, u32[]{:S(2)}, u32[]{:S(2)}) collective-permute-start(f32[8,16384]{1,0:T(8,128)S(1)} %update.25.refs_0_), channel_id=1, source_target_pairs={{0,16},{16,32},{32,48},{48,64},{64,80},{80,96},{96,112},{112,128},... | collective-permute-start | bytes 1572872 | tf_op jit(solution)/shard_map/ppermute | solution.py:197
  307.2 13.9 %collective-permute-start.72 = (f32[8,128]{1,0:T(8,128)S(1)}, f32[8,128]{1,0:T(8,128)S(1)}, u32[]{:S(2)}, u32[]{:S(2)}) collective-permute-start(f32[8,128]{1,0:T(8,128)S(1)} %product.40), channel_id=1, source_target_pairs={{0,16},{16,32},{32,48},{48,64},{64,80},{80,96},{96,112},{112,128},... | collective-permute-start | bytes 12296 | tf_op jit(solution)/shard_map/ppermute | solution.py:197
  307.3 14.0 %collective-permute-start.73 = (f32[8,128]{1,0:T(8,128)S(1)}, f32[8,128]{1,0:T(8,128)S(1)}, u32[]{:S(2)}, u32[]{:S(2)}) collective-permute-start(f32[8,128]{1,0:T(8,128)S(1)} %product.40), channel_id=1, source_target_pairs={{0,24},{1,25},{2,26},{3,27},{4,28},{5,29},{6,30},{7,31},{8,16},{9,... | collective-permute-start | bytes 12296 | tf_op jit(solution)/shard_map/ppermute | solution.py:203
  334.5 24.4 %collective-permute-start.83 = (f32[8,16384]{1,0:T(8,128)S(1)}, f32[8,16384]{1,0:T(8,128)S(1)}, u32[]{:S(2)}, u32[]{:S(2)}) collective-permute-start(f32[8,16384]{1,0:T(8,128)S(1)} %update.26.refs_0_), channel_id=1, source_target_pairs={{0,16},{16,32},{32,48},{48,64},{64,80},{80,96},{96,112},{112,128},... | collective-permute-start | bytes 1572872 | tf_op jit(solution)/shard_map/ppermute | solution.py:197
  334.5 13.9 %collective-permute-start.78 = (f32[8,128]{1,0:T(8,128)S(1)}, f32[8,128]{1,0:T(8,128)S(1)}, u32[]{:S(2)}, u32[]{:S(2)}) collective-permute-start(f32[8,128]{1,0:T(8,128)S(1)} %product.41), channel_id=1, source_target_pairs={{0,16},{16,32},{32,48},{48,64},{64,80},{80,96},{96,112},{112,128},... | collective-permute-start | bytes 12296 | tf_op jit(solution)/shard_map/ppermute | solution.py:197
  334.6 14.4 %collective-permute-start.79 = (f32[8,128]{1,0:T(8,128)S(1)}, f32[8,128]{1,0:T(8,128)S(1)}, u32[]{:S(2)}, u32[]{:S(2)}) collective-permute-start(f32[8,128]{1,0:T(8,128)S(1)} %product.41), channel_id=1, source_target_pairs={{0,24},{1,25},{2,26},{3,27},{4,28},{5,29},{6,30},{7,31},{8,16},{9,... | collective-permute-start | bytes 12296 | tf_op jit(solution)/shard_map/ppermute | solution.py:203
  362.0 24.0 %collective-permute-start.89 = (f32[8,16384]{1,0:T(8,128)S(1)}, f32[8,16384]{1,0:T(8,128)S(1)}, u32[]{:S(2)}, u32[]{:S(2)}) collective-permute-start(f32[8,16384]{1,0:T(8,128)S(1)} %update.27.refs_0_), channel_id=1, source_target_pairs={{0,16},{16,32},{32,48},{48,64},{64,80},{80,96},{96,112},{112,128},... | collective-permute-start | bytes 1572872 | tf_op jit(solution)/shard_map/ppermute | solution.py:197
  362.1 13.9 %collective-permute-start.84 = (f32[8,128]{1,0:T(8,128)S(1)}, f32[8,128]{1,0:T(8,128)S(1)}, u32[]{:S(2)}, u32[]{:S(2)}) collective-permute-start(f32[8,128]{1,0:T(8,128)S(1)} %product.42), channel_id=1, source_target_pairs={{0,16},{16,32},{32,48},{48,64},{64,80},{80,96},{96,112},{112,128},... | collective-permute-start | bytes 12296 | tf_op jit(solution)/shard_map/ppermute | solution.py:197
  362.2 14.0 %collective-permute-start.85 = (f32[8,128]{1,0:T(8,128)S(1)}, f32[8,128]{1,0:T(8,128)S(1)}, u32[]{:S(2)}, u32[]{:S(2)}) collective-permute-start(f32[8,128]{1,0:T(8,128)S(1)} %product.42), channel_id=1, source_target_pairs={{0,24},{1,25},{2,26},{3,27},{4,28},{5,29},{6,30},{7,31},{8,16},{9,... | collective-permute-start | bytes 12296 | tf_op jit(solution)/shard_map/ppermute | solution.py:203
  389.2 24.4 %collective-permute-start.95 = (f32[8,16384]{1,0:T(8,128)S(1)}, f32[8,16384]{1,0:T(8,128)S(1)}, u32[]{:S(2)}, u32[]{:S(2)}) collective-permute-start(f32[8,16384]{1,0:T(8,128)S(1)} %update.28.refs_0_), channel_id=1, source_target_pairs={{0,16},{16,32},{32,48},{48,64},{64,80},{80,96},{96,112},{112,128},... | collective-permute-start | bytes 1572872 | tf_op jit(solution)/shard_map/ppermute | solution.py:197
  389.2 13.9 %collective-permute-start.90 = (f32[8,128]{1,0:T(8,128)S(1)}, f32[8,128]{1,0:T(8,128)S(1)}, u32[]{:S(2)}, u32[]{:S(2)}) collective-permute-start(f32[8,128]{1,0:T(8,128)S(1)} %product.43), channel_id=1, source_target_pairs={{0,16},{16,32},{32,48},{48,64},{64,80},{80,96},{96,112},{112,128},... | collective-permute-start | bytes 12296 | tf_op jit(solution)/shard_map/ppermute | solution.py:197
  389.3 14.4 %collective-permute-start.91 = (f32[8,128]{1,0:T(8,128)S(1)}, f32[8,128]{1,0:T(8,128)S(1)}, u32[]{:S(2)}, u32[]{:S(2)}) collective-permute-start(f32[8,128]{1,0:T(8,128)S(1)} %product.43), channel_id=1, source_target_pairs={{0,24},{1,25},{2,26},{3,27},{4,28},{5,29},{6,30},{7,31},{8,16},{9,... | collective-permute-start | bytes 12296 | tf_op jit(solution)/shard_map/ppermute | solution.py:203
  416.7 24.0 %collective-permute-start.101 = (f32[8,16384]{1,0:T(8,128)S(1)}, f32[8,16384]{1,0:T(8,128)S(1)}, u32[]{:S(2)}, u32[]{:S(2)}) collective-permute-start(f32[8,16384]{1,0:T(8,128)S(1)} %update.29.refs_0_), channel_id=1, source_target_pairs={{0,16},{16,32},{32,48},{48,64},{64,80},{80,96},{96,112},{112,128},... | collective-permute-start | bytes 1572872 | tf_op jit(solution)/shard_map/ppermute | solution.py:197
  416.8 13.9 %collective-permute-start.96 = (f32[8,128]{1,0:T(8,128)S(1)}, f32[8,128]{1,0:T(8,128)S(1)}, u32[]{:S(2)}, u32[]{:S(2)}) collective-permute-start(f32[8,128]{1,0:T(8,128)S(1)} %product.44), channel_id=1, source_target_pairs={{0,16},{16,32},{32,48},{48,64},{64,80},{80,96},{96,112},{112,128},... | collective-permute-start | bytes 12296 | tf_op jit(solution)/shard_map/ppermute | solution.py:197
  416.9 14.0 %collective-permute-start.97 = (f32[8,128]{1,0:T(8,128)S(1)}, f32[8,128]{1,0:T(8,128)S(1)}, u32[]{:S(2)}, u32[]{:S(2)}) collective-permute-start(f32[8,128]{1,0:T(8,128)S(1)} %product.44), channel_id=1, source_target_pairs={{0,24},{1,25},{2,26},{3,27},{4,28},{5,29},{6,30},{7,31},{8,16},{9,... | collective-permute-start | bytes 12296 | tf_op jit(solution)/shard_map/ppermute | solution.py:203
  443.9 24.4 %collective-permute-start.107 = (f32[8,16384]{1,0:T(8,128)S(1)}, f32[8,16384]{1,0:T(8,128)S(1)}, u32[]{:S(2)}, u32[]{:S(2)}) collective-permute-start(f32[8,16384]{1,0:T(8,128)S(1)} %update.30.refs_0_), channel_id=1, source_target_pairs={{0,16},{16,32},{32,48},{48,64},{64,80},{80,96},{96,112},{112,128},... | collective-permute-start | bytes 1572872 | tf_op jit(solution)/shard_map/ppermute | solution.py:197
  443.9 13.9 %collective-permute-start.102 = (f32[8,128]{1,0:T(8,128)S(1)}, f32[8,128]{1,0:T(8,128)S(1)}, u32[]{:S(2)}, u32[]{:S(2)}) collective-permute-start(f32[8,128]{1,0:T(8,128)S(1)} %product.45), channel_id=1, source_target_pairs={{0,16},{16,32},{32,48},{48,64},{64,80},{80,96},{96,112},{112,128},... | collective-permute-start | bytes 12296 | tf_op jit(solution)/shard_map/ppermute | solution.py:197
  444.0 14.4 %collective-permute-start.103 = (f32[8,128]{1,0:T(8,128)S(1)}, f32[8,128]{1,0:T(8,128)S(1)}, u32[]{:S(2)}, u32[]{:S(2)}) collective-permute-start(f32[8,128]{1,0:T(8,128)S(1)} %product.45), channel_id=1, source_target_pairs={{0,24},{1,25},{2,26},{3,27},{4,28},{5,29},{6,30},{7,31},{8,16},{9,... | collective-permute-start | bytes 12296 | tf_op jit(solution)/shard_map/ppermute | solution.py:203
  469.9 13.9 %collective-permute-start.108 = (f32[8,16384]{1,0:T(8,128)S(1)}, f32[8,16384]{1,0:T(8,128)S(1)}, u32[]{:S(2)}, u32[]{:S(2)}) collective-permute-start(f32[8,16384]{1,0:T(8,128)S(1)} %update.31), channel_id=1, source_target_pairs={{0,16},{16,32},{32,48},{48,64},{64,80},{80,96},{96,112},{112,128},... | collective-permute-start | bytes 1572872 | tf_op jit(solution)/shard_map/ppermute | solution.py:197
  (64 other events, 252.5 us)

commit v3 on v2

--- a/solution.py
+++ b/solution.py
@@ -118,31 +118,35 @@
     lax.fori_loop(low, high, step, 0, unroll=2 if (high - low) % 2 == 0 else 1)
 
 
-def product_kernel(first, turned, add, *refs):
-    x_ref, a_ref = refs[0], refs[1]
+def product_kernel(first, turned, pieces, add, *refs):
+    a_ref = refs[pieces]
     o_ref, acc = refs[-2], refs[-1]
     acc[...] = jnp.zeros_like(acc)
-
-    def step(c, _):
-        lhs = jnp.concatenate(parts_of(x_ref[:, at(c)]), axis=0)
-        if turned:
-            acc[...] += jnp.dot(lhs, a_ref[c + first], preferred_element_type=f32)
-        else:
-            acc[...] += lax.dot_general(
-                lhs, a_ref[c + first], (((1,), (1,)), ((), ())), preferred_element_type=f32
-            )
-        return 0
-
-    looped(0, x_ref.shape[1] // CHUNK, step)
+    begin = first
+    for x_ref in refs[:pieces]:
+
+        def step(c, _, x_ref=x_ref, begin=begin):
+            lhs = jnp.concatenate(parts_of(x_ref[:, at(c)]), axis=0)
+            if turned:
+                acc[...] += jnp.dot(lhs, a_ref[c + begin], preferred_element_type=f32)
+            else:
+                acc[...] += lax.dot_general(
+                    lhs, a_ref[c + begin], (((1,), (1,)), ((), ())), preferred_element_type=f32
+                )
+            return 0
+
+        count = x_ref.shape[1] // CHUNK
+        looped(0, count, step)
+        begin += count
     both = acc[0:8, :] + acc[8:16, :]
     p = both[:, :128] + both[:, 128:]
-    o_ref[...] = p + refs[2][...] if add else p
-
-
-def product(x, a, first, turned, before):
-    operands = [x, a] + ([] if before is None else [before])
-    return pl.pallas_call(
-        functools.partial(product_kernel, first, turned, before is not None),
+    o_ref[...] = p + refs[pieces + 1][...] if add else p
+
+
+def product(xs, a, first, turned, before):
+    operands = [*xs, a] + ([] if before is None else [before])
+    return pl.pallas_call(
+        functools.partial(product_kernel, first, turned, len(xs), before is not None),
         in_specs=[VMEM] * len(operands),
         out_specs=VMEM,
         out_shape=jax.ShapeDtypeStruct((8, 128), f32),
@@ -203,13 +207,24 @@
     return lax.ppermute(block, ("rows", "vox"), pairs)
 
 
-def exchanged(p, reach):
+def from_partner(p, reach):
     n = lax.axis_size("vox")
-    return p + lax.ppermute(p, "vox", [(i, i ^ reach) for i in range(n)])
-
-
-def ends(held, n):
-    return tuple(e for e in (held, n) if e > 0) if held < n else (n,)
+    return lax.ppermute(p, "vox", [(i, i ^ reach) for i in range(n)])
+
+
+def summed_four(p):
+    c = from_partner(p, 4)
+    b = from_partner(p, 2)
+    d = from_partner(p, 6)
+    return (p + b) + (c + d)
+
+
+def ends(held, n, last):
+    if last or held == n:
+        return (2, 4, n), 3
+    far = n - held
+    cuts = (held + far // 2, n) if far > 3 else (n,)
+    return ((held, *cuts), 1) if held else (cuts, 0)
 
 
 def shards(system, measured, start_image):
@@ -220,46 +235,50 @@
     arriving = []
     following = None
     pieces, ins, held, crossed = [start_image], (n,), 0, False
-    p = product(start_image, own, 0, False, None)
+    p = product(pieces, own, 0, False, None)
     for k in range(cycle):
         last = k == cycle - 1
         now = 0 if last else HELD[k]
-        outs = ends(now, n)
+        outs, count = ends(now, n, last)
         if not crossed:
-            p = exchanged(p, 8)
+            p = p + from_partner(p, 8)
         if len(arriving) < n and not last:
             p, chunk = barrier((p, chunks[len(arriving)]))
             arriving.append(shifted(chunk, -1))
-        p = exchanged(p, 1)
-        for reach in (2, 4):
-            p = exchanged(p, reach)
+        p = p + from_partner(p, 1)
+        p = summed_four(p)
         new = update(k, p, wanted, own, pieces, ins, outs)
+        ins = outs
         if last:
-            return shifted(new[0], 1)
+            return jnp.concatenate([shifted(x, 1) for x in new], axis=1)
         if now < n:
-            far = shifted(new[-1], 1)
+            far = [shifted(x, 1) for x in new[count:]]
         for c in range(held, now):
             following = split_turned(c, gate(arriving[c], p), following)
         held = now
         if now == 0:
-            pieces = [far]
+            pieces = far
             p = product(far, own, 0, False, None)
+            continue
+        crossed = now == n
+        if crossed:
+            first = [shifted(new[0], 1)]
+            rest = new[1:]
+            p = product(new, following, 0, True, None)
         else:
-            p = product(new[0], following, 0, True, None)
-            p, kept = barrier((p, new[0]))
-            crossed = now == n
-            if crossed:
-                across = shifted_across(p, 8)
-            p = shifted(p, 1)
-            if crossed:
-                p = p + across
-            near = shifted(kept, 1)
-            if now < n:
-                p = product(far, own, now, False, p)
-                pieces = [near, far]
-            else:
-                pieces = [near]
-        ins = outs
+            first, rest = [], new[:count]
+            p = product(rest, following, 0, True, None)
+        p, *rest = barrier((p, *rest))
+        if crossed:
+            across = shifted_across(p, 8)
+        p = shifted(p, 1)
+        near = first + [shifted(x, 1) for x in rest]
+        if crossed:
+            p = p + across
+            pieces = near
+        else:
+            p = product(far, own, now, False, p)
+            pieces = near + far
 
 
 def solution(mesh):

time: 494 us -> 499 us (1.010)
  the two profiles are of different devices: /device:TPU:8 before, /device:TPU:1 now
where the time goes in v3:
time: 499 us; the launch traced here: 489 us
  waiting for transfers between devices  270 us (54%)
  starting transfers between devices  153 us (31%)
  Pallas kernels  61 us (12%)
    ppermute x66, waiting for transfers between devices, shifted(): lax.ppermute(block, 'rows', [(i, (i + distance) % n) for i in range(n)])  197 us
    ppermute x73, starting transfers between devices, from_partner(): return lax.ppermute(p, 'vox', [(i, i ^ reach) for i in range(n)])  130 us
    ppermute x73, waiting for transfers between devices, from_partner(): return lax.ppermute(p, 'vox', [(i, i ^ reach) for i in range(n)])  70.4 us
    pallas_call x23, Pallas kernels, product(): pl.pallas_call(functools.partial(product_kernel, first, turned, len(xs),...  32 us
    pallas_call x16, Pallas kernels, update(): pl.pallas_call(functools.partial(update_kernel, k, ins, outs), in_specs=[...  24.4 us
    ppermute x66, starting transfers between devices, shifted(): lax.ppermute(block, 'rows', [(i, (i + distance) % n) for i in range(n)])  22.2 us
  transfers between devices with their start and end apart: 146, of which 100 were waited for; matrix products, arithmetic and copies ran while one was open for 0% of the time, Pallas kernels for 7%

profile of v3, /device:TPU:1, one launch (start us, length us, event | category | flops | bytes accessed | tf_op | source)
XLA Modules:
  0.0 489.3 jit_solution(14383002214971963103)
XLA Ops:
  0.0 3.4 copy-done
  7.8 3.6 collective-permute-start
  12.4 3.8 collective-permute-start.1
  19.7 5.9 %collective-permute-start.14 = (f32[128,2048]{1,0:T(8,128)S(1)}, f32[128,2048]{1,0:T(8,128)S(1)}, u32[]{:S(2)}, u32[]{:S(2)}) collective-permute-start(f32[128,2048]{1,0:T(8,128)S(1)} %get-tuple-element.127), channel_id=1, source_target_pairs={{0,240},{16,0},{32,16},{48,32},{64,48},{80,64},{96,80},{112,96},{1... | collective-permute-start | bytes 3145736 | tf_op jit(solution)/shard_map/ppermute | solution.py:201
  27.4 8.7 %collective-permute-done.5.refs_0_ = f32[8,8192]{1,0:T(8,128)S(1)} collective-permute-done((f32[8,8192]{1,0:T(8,128)S(1)}, f32[8,8192]{1,0:T(8,128)S(1)}, u32[]{:S(2)}, u32[]{:S(2)}) %collective-permute-start.5) | collective-permute-done | bytes 262176 | tf_op jit(solution)/shard_map/ppermute | solution.py:201
  36.1 5.6 %collective-permute-done.6.refs_1_ = f32[8,8192]{1,0:T(8,128)S(1)} collective-permute-done((f32[8,8192]{1,0:T(8,128)S(1)}, f32[8,8192]{1,0:T(8,128)S(1)}, u32[]{:S(2)}, u32[]{:S(2)}) %collective-permute-start.6) | collective-permute-done | bytes 262176 | tf_op jit(solution)/shard_map/ppermute | solution.py:201
  49.1 3.7 collective-permute-start.8
  63.8 9.6 %collective-permute-done.12.refs_0_.refs_1_ = f32[8,6144]{1,0:T(8,128)S(1)} collective-permute-done((f32[8,6144]{1,0:T(8,128)S(1)}, f32[8,6144]{1,0:T(8,128)S(1)}, u32[]{:S(2)}, u32[]{:S(2)}) %collective-permute-start.12) | collective-permute-done | bytes 196640 | tf_op jit(solution)/shard_map/ppermute | solution.py:201
  80.0 3.8 collective-permute-start.17
  89.8 4.0 collective-permute-done.21.refs_0_
  96.3 5.8 %collective-permute-done.22.refs_0_.refs_1_ = f32[8,6144]{1,0:T(8,128)S(1)} collective-permute-done((f32[8,6144]{1,0:T(8,128)S(1)}, f32[8,6144]{1,0:T(8,128)S(1)}, u32[]{:S(2)}, u32[]{:S(2)}) %collective-permute-start.22) | collective-permute-done | bytes 196640 | tf_op jit(solution)/shard_map/ppermute | solution.py:201
  102.0 3.5 collective-permute-done.23.refs_1_.refs_2_
  112.1 4.8 collective-permute-start.27
  123.4 4.2 collective-permute-done.31.refs_0_
  130.5 7.4 %collective-permute-done.32.refs_0_.refs_1_ = f32[8,4096]{1,0:T(8,128)S(1)} collective-permute-done((f32[8,4096]{1,0:T(8,128)S(1)}, f32[8,4096]{1,0:T(8,128)S(1)}, u32[]{:S(2)}, u32[]{:S(2)}) %collective-permute-start.32) | collective-permute-done | bytes 131104 | tf_op jit(solution)/shard_map/ppermute | solution.py:201
  143.9 4.6 collective-permute-start.37
  155.1 5.3 %collective-permute-done.41.refs_0_ = f32[8,6144]{1,0:T(8,128)S(1)} collective-permute-done((f32[8,6144]{1,0:T(8,128)S(1)}, f32[8,6144]{1,0:T(8,128)S(1)}, u32[]{:S(2)}, u32[]{:S(2)}) %collective-permute-start.41) | collective-permute-done | bytes 196640 | tf_op jit(solution)/shard_map/ppermute | solution.py:201
  163.8 6.4 %collective-permute-done.45.refs_3_ = f32[8,128]{1,0:T(8,128)S(1)} collective-permute-done((f32[8,128]{1,0:T(8,128)S(1)}, f32[8,128]{1,0:T(8,128)S(1)}, u32[]{:S(2)}, u32[]{:S(2)}) %collective-permute-start.45) | collective-permute-done | bytes 4128 | tf_op jit(solution)/shard_map/ppermute | solution.py:201
  176.8 4.9 %collective-permute-start.47 = (f32[8,128]{1,0:T(8,128)S(1)}, f32[8,128]{1,0:T(8,128)S(1)}, u32[]{:S(2)}, u32[]{:S(2)}) collective-permute-start(f32[8,128]{1,0:T(8,128)S(1)} %add.265), channel_id=1, source_target_pairs={{0,1},{1,0},{2,3},{3,2},{4,5},{5,4},{6,7},{7,6},{8,9},{9,8},{10,11... | collective-permute-start | bytes 12296 | tf_op jit(solution)/shard_map/ppermute | solution.py:212
  192.9 4.8 collective-permute-done.52.refs_0_.refs_1_
  204.5 5.3 %collective-permute-start.56 = (f32[8,128]{1,0:T(8,128)S(1)}, f32[8,128]{1,0:T(8,128)S(1)}, u32[]{:S(2)}, u32[]{:S(2)}) collective-permute-start(f32[8,128]{1,0:T(8,128)S(1)} %add.270), channel_id=1, source_target_pairs={{0,1},{1,0},{2,3},{3,2},{4,5},{5,4},{6,7},{7,6},{8,9},{9,8},{10,11... | collective-permute-start | bytes 12296 | tf_op jit(solution)/shard_map/ppermute | solution.py:212
  222.4 4.9 collective-permute-done.63.refs_2_
  233.4 5.1 %collective-permute-start.65 = (f32[8,128]{1,0:T(8,128)S(1)}, f32[8,128]{1,0:T(8,128)S(1)}, u32[]{:S(2)}, u32[]{:S(2)}) collective-permute-start(f32[8,128]{1,0:T(8,128)S(1)} %add.275), channel_id=1, source_target_pairs={{0,1},{1,0},{2,3},{3,2},{4,5},{5,4},{6,7},{7,6},{8,9},{9,8},{10,11... | collective-permute-start | bytes 12296 | tf_op jit(solution)/shard_map/ppermute | solution.py:212
  250.6 13.1 %collective-permute-done.70.refs_0_.refs_1_ = f32[8,2048]{1,0:T(8,128)S(1)} collective-permute-done((f32[8,2048]{1,0:T(8,128)S(1)}, f32[8,2048]{1,0:T(8,128)S(1)}, u32[]{:S(2)}, u32[]{:S(2)}) %collective-permute-start.70) | collective-permute-done | bytes 65568 | tf_op jit(solution)/shard_map/ppermute | solution.py:201
  268.1 4.1 collective-permute-start.74
  282.0 8.0 %collective-permute-done.80 = f32[8,128]{1,0:T(8,128)S(1)} collective-permute-done((f32[8,128]{1,0:T(8,128)S(1)}, f32[8,128]{1,0:T(8,128)S(1)}, u32[]{:S(2)}, u32[]{:S(2)}) %collective-permute-start.80) | collective-permute-done | bytes 4128 | tf_op jit(solution)/shard_map/ppermute | solution.py:201
  291.1 2.9 collective-permute-start.82
  300.2 3.3 collective-permute-done.86.refs_0_
  303.4 3.4 collective-permute-done.87.refs_1_
  310.0 8.1 %collective-permute-done.89 = f32[8,128]{1,0:T(8,128)S(1)} collective-permute-done((f32[8,128]{1,0:T(8,128)S(1)}, f32[8,128]{1,0:T(8,128)S(1)}, u32[]{:S(2)}, u32[]{:S(2)}) %collective-permute-start.89) | collective-permute-done | bytes 4128 | tf_op jit(solution)/shard_map/ppermute | solution.py:201
  327.5 3.3 collective-permute-done.95.refs_0_
  336.7 8.1 %collective-permute-done.98 = f32[8,128]{1,0:T(8,128)S(1)} collective-permute-done((f32[8,128]{1,0:T(8,128)S(1)}, f32[8,128]{1,0:T(8,128)S(1)}, u32[]{:S(2)}, u32[]{:S(2)}) %collective-permute-start.98) | collective-permute-done | bytes 4128 | tf_op jit(solution)/shard_map/ppermute | solution.py:201
  345.3 2.9 collective-permute-start.100
  349.0 3.0 collective-permute-start.102
  355.7 3.3 collective-permute-done.104.refs_0_
  364.9 8.1 %collective-permute-done.107 = f32[8,128]{1,0:T(8,128)S(1)} collective-permute-done((f32[8,128]{1,0:T(8,128)S(1)}, f32[8,128]{1,0:T(8,128)S(1)}, u32[]{:S(2)}, u32[]{:S(2)}) %collective-permute-start.107) | collective-permute-done | bytes 4128 | tf_op jit(solution)/shard_map/ppermute | solution.py:201
  376.5 2.9 collective-permute-start.111
  383.1 3.3 collective-permute-done.113.refs_0_
  392.5 7.9 %collective-permute-done.116 = f32[8,128]{1,0:T(8,128)S(1)} collective-permute-done((f32[8,128]{1,0:T(8,128)S(1)}, f32[8,128]{1,0:T(8,128)S(1)}, u32[]{:S(2)}, u32[]{:S(2)}) %collective-permute-start.116) | collective-permute-done | bytes 4128 | tf_op jit(solution)/shard_map/ppermute | solution.py:201
  400.8 2.9 collective-permute-start.118
  404.6 2.9 collective-permute-start.120
  411.2 3.3 collective-permute-done.122.refs_0_
  420.4 8.1 %collective-permute-done.125 = f32[8,128]{1,0:T(8,128)S(1)} collective-permute-done((f32[8,128]{1,0:T(8,128)S(1)}, f32[8,128]{1,0:T(8,128)S(1)}, u32[]{:S(2)}, u32[]{:S(2)}) %collective-permute-start.125) | collective-permute-done | bytes 4128 | tf_op jit(solution)/shard_map/ppermute | solution.py:201
  438.5 3.3 collective-permute-done.131.refs_0_
  447.7 8.1 %collective-permute-done.134 = f32[8,128]{1,0:T(8,128)S(1)} collective-permute-done((f32[8,128]{1,0:T(8,128)S(1)}, f32[8,128]{1,0:T(8,128)S(1)}, u32[]{:S(2)}, u32[]{:S(2)}) %collective-permute-start.134) | collective-permute-done | bytes 4128 | tf_op jit(solution)/shard_map/ppermute | solution.py:201
  456.3 2.9 collective-permute-start.136
  466.6 3.3 collective-permute-done.140.refs_0_
  474.4 10.8 %collective-permute-done.144 = f32[8,4096]{1,0:T(8,128)S(1)} collective-permute-done((f32[8,4096]{1,0:T(8,128)S(1)}, f32[8,4096]{1,0:T(8,128)S(1)}, u32[]{:S(2)}, u32[]{:S(2)}) %collective-permute-start.144) | collective-permute-done | bytes 131104 | tf_op jit(solution)/shard_map/ppermute | solution.py:201
  (348 shorter events, 237.7 us)
Async XLA Ops:
  17.0 8.6 %collective-permute-start.3 = (f32[8,128]{1,0:T(8,128)S(1)}, f32[8,128]{1,0:T(8,128)S(1)}, u32[]{:S(2)}, u32[]{:S(2)}) collective-permute-start(f32[8,128]{1,0:T(8,128)S(1)} %add.241), channel_id=1, source_target_pairs={{0,4},{1,5},{2,6},{3,7},{4,0},{5,1},{6,2},{7,3},{8,12},{9,13},{10,... | collective-permute-start | bytes 12296 | tf_op jit(solution)/shard_map/ppermute | solution.py:212
  19.7 43.5 %collective-permute-start.14 = (f32[128,2048]{1,0:T(8,128)S(1)}, f32[128,2048]{1,0:T(8,128)S(1)}, u32[]{:S(2)}, u32[]{:S(2)}) collective-permute-start(f32[128,2048]{1,0:T(8,128)S(1)} %get-tuple-element.127), channel_id=1, source_target_pairs={{0,240},{16,0},{32,16},{48,32},{64,48},{80,64},{96,80},{112,96},{1... | collective-permute-start | bytes 3145736 | tf_op jit(solution)/shard_map/ppermute | solution.py:201
  27.2 8.9 %collective-permute-start.5 = (f32[8,8192]{1,0:T(8,128)S(1)}, f32[8,8192]{1,0:T(8,128)S(1)}, u32[]{:S(2)}, u32[]{:S(2)}) collective-permute-start(f32[8,8192]{1,0:T(8,128)S(1)} %get-tuple-element.120), channel_id=1, source_target_pairs={{0,16},{16,32},{32,48},{48,64},{64,80},{80,96},{96,112},{112,128},... | collective-permute-start | bytes 786440 | tf_op jit(solution)/shard_map/ppermute | solution.py:201
  27.3 14.4 %collective-permute-start.6 = (f32[8,8192]{1,0:T(8,128)S(1)}, f32[8,8192]{1,0:T(8,128)S(1)}, u32[]{:S(2)}, u32[]{:S(2)}) collective-permute-start(f32[8,8192]{1,0:T(8,128)S(1)} %get-tuple-element.121), channel_id=1, source_target_pairs={{0,16},{16,32},{32,48},{48,64},{64,80},{80,96},{96,112},{112,128},... | collective-permute-start | bytes 786440 | tf_op jit(solution)/shard_map/ppermute | solution.py:201
  48.3 47.2 %collective-permute-start.24 = (f32[128,2048]{1,0:T(8,128)S(1)}, f32[128,2048]{1,0:T(8,128)S(1)}, u32[]{:S(2)}, u32[]{:S(2)}) collective-permute-start(f32[128,2048]{1,0:T(8,128)S(1)} %get-tuple-element.136), channel_id=1, source_target_pairs={{0,240},{16,0},{32,16},{48,32},{64,48},{80,64},{96,80},{112,96},{1... | collective-permute-start | bytes 3145736 | tf_op jit(solution)/shard_map/ppermute | solution.py:201
  60.9 12.5 %collective-permute-start.13 = (f32[8,8192]{1,0:T(8,128)S(1)}, f32[8,8192]{1,0:T(8,128)S(1)}, u32[]{:S(2)}, u32[]{:S(2)}) collective-permute-start(f32[8,8192]{1,0:T(8,128)S(1)} %get-tuple-element.125), channel_id=1, source_target_pairs={{0,16},{16,32},{32,48},{48,64},{64,80},{80,96},{96,112},{112,128},... | collective-permute-start | bytes 786440 | tf_op jit(solution)/shard_map/ppermute | solution.py:201
  62.7 10.7 %collective-permute-start.12 = (f32[8,6144]{1,0:T(8,128)S(1)}, f32[8,6144]{1,0:T(8,128)S(1)}, u32[]{:S(2)}, u32[]{:S(2)}) collective-permute-start(f32[8,6144]{1,0:T(8,128)S(1)} %get-tuple-element.124), channel_id=1, source_target_pairs={{0,16},{16,32},{32,48},{48,64},{64,80},{80,96},{96,112},{112,128},... | collective-permute-start | bytes 589832 | tf_op jit(solution)/shard_map/ppermute | solution.py:201
  63.8 9.7 %collective-permute-start.15 = (f32[8,128]{1,0:T(8,128)S(1)}, f32[8,128]{1,0:T(8,128)S(1)}, u32[]{:S(2)}, u32[]{:S(2)}) collective-permute-start(f32[8,128]{1,0:T(8,128)S(1)} %product.25), channel_id=1, source_target_pairs={{0,16},{16,32},{32,48},{48,64},{64,80},{80,96},{96,112},{112,128},... | collective-permute-start | bytes 12296 | tf_op jit(solution)/shard_map/ppermute | solution.py:201
  83.8 45.5 %collective-permute-start.34 = (f32[128,2048]{1,0:T(8,128)S(1)}, f32[128,2048]{1,0:T(8,128)S(1)}, u32[]{:S(2)}, u32[]{:S(2)}) collective-permute-start(f32[128,2048]{1,0:T(8,128)S(1)} %get-tuple-element.145), channel_id=1, source_target_pairs={{0,240},{16,0},{32,16},{48,32},{64,48},{80,64},{96,80},{112,96},{1... | collective-permute-start | bytes 3145736 | tf_op jit(solution)/shard_map/ppermute | solution.py:201
  95.4 10.1 %collective-permute-start.23 = (f32[8,6144]{1,0:T(8,128)S(1)}, f32[8,6144]{1,0:T(8,128)S(1)}, u32[]{:S(2)}, u32[]{:S(2)}) collective-permute-start(f32[8,6144]{1,0:T(8,128)S(1)} %get-tuple-element.134), channel_id=1, source_target_pairs={{0,16},{16,32},{32,48},{48,64},{64,80},{80,96},{96,112},{112,128},... | collective-permute-start | bytes 589832 | tf_op jit(solution)/shard_map/ppermute | solution.py:201
  96.3 9.4 %collective-permute-start.25 = (f32[8,128]{1,0:T(8,128)S(1)}, f32[8,128]{1,0:T(8,128)S(1)}, u32[]{:S(2)}, u32[]{:S(2)}) collective-permute-start(f32[8,128]{1,0:T(8,128)S(1)} %product.27), channel_id=1, source_target_pairs={{0,16},{16,32},{32,48},{48,64},{64,80},{80,96},{96,112},{112,128},... | collective-permute-start | bytes 12296 | tf_op jit(solution)/shard_map/ppermute | solution.py:201
  112.0 50.5 %collective-permute-start.44 = (f32[128,2048]{1,0:T(8,128)S(1)}, f32[128,2048]{1,0:T(8,128)S(1)}, u32[]{:S(2)}, u32[]{:S(2)}) collective-permute-start(f32[128,2048]{1,0:T(8,128)S(1)} %get-tuple-element.154), channel_id=1, source_target_pairs={{0,240},{16,0},{32,16},{48,32},{64,48},{80,64},{96,80},{112,96},{1... | collective-permute-start | bytes 3145736 | tf_op jit(solution)/shard_map/ppermute | solution.py:201
  129.1 8.8 %collective-permute-start.33 = (f32[8,6144]{1,0:T(8,128)S(1)}, f32[8,6144]{1,0:T(8,128)S(1)}, u32[]{:S(2)}, u32[]{:S(2)}) collective-permute-start(f32[8,6144]{1,0:T(8,128)S(1)} %get-tuple-element.143), channel_id=1, source_target_pairs={{0,16},{16,32},{32,48},{48,64},{64,80},{80,96},{96,112},{112,128},... | collective-permute-start | bytes 589832 | tf_op jit(solution)/shard_map/ppermute | solution.py:201
  129.2 8.7 %collective-permute-start.32 = (f32[8,4096]{1,0:T(8,128)S(1)}, f32[8,4096]{1,0:T(8,128)S(1)}, u32[]{:S(2)}, u32[]{:S(2)}) collective-permute-start(f32[8,4096]{1,0:T(8,128)S(1)} %get-tuple-element.142), channel_id=1, source_target_pairs={{0,16},{16,32},{32,48},{48,64},{64,80},{80,96},{96,112},{112,128},... | collective-permute-start | bytes 393224 | tf_op jit(solution)/shard_map/ppermute | solution.py:201
  143.9 47.2 %collective-permute-start.53 = (f32[128,2048]{1,0:T(8,128)S(1)}, f32[128,2048]{1,0:T(8,128)S(1)}, u32[]{:S(2)}, u32[]{:S(2)}) collective-permute-start(f32[128,2048]{1,0:T(8,128)S(1)} %get-tuple-element.162), channel_id=1, source_target_pairs={{0,240},{16,0},{32,16},{48,32},{64,48},{80,64},{96,80},{112,96},{1... | collective-permute-start | bytes 3145736 | tf_op jit(solution)/shard_map/ppermute | solution.py:201
  175.4 45.5 %collective-permute-start.62 = (f32[128,2048]{1,0:T(8,128)S(1)}, f32[128,2048]{1,0:T(8,128)S(1)}, u32[]{:S(2)}, u32[]{:S(2)}) collective-permute-start(f32[128,2048]{1,0:T(8,128)S(1)} %get-tuple-element.170), channel_id=1, source_target_pairs={{0,240},{16,0},{32,16},{48,32},{64,48},{80,64},{96,80},{112,96},{1... | collective-permute-start | bytes 3145736 | tf_op jit(solution)/shard_map/ppermute | solution.py:201
  175.4 14.2 %collective-permute-start.51 = (f32[8,8192]{1,0:T(8,128)S(1)}, f32[8,8192]{1,0:T(8,128)S(1)}, u32[]{:S(2)}, u32[]{:S(2)}) collective-permute-start(f32[8,8192]{1,0:T(8,128)S(1)} %get-tuple-element.159.refs_0_), channel_id=1, source_target_pairs={{0,16},{16,32},{32,48},{48,64},{64,80},{80,96},{96,112},{112,128},... | collective-permute-start | bytes 786440 | tf_op jit(solution)/shard_map/ppermute | solution.py:201
  192.8 24.6 %collective-permute-start.60 = (f32[8,10240]{1,0:T(8,128)S(1)}, f32[8,10240]{1,0:T(8,128)S(1)}, u32[]{:S(2)}, u32[]{:S(2)}) collective-permute-start(f32[8,10240]{1,0:T(8,128)S(1)} %get-tuple-element.167.refs_0_), channel_id=1, source_target_pairs={{0,16},{16,32},{32,48},{48,64},{64,80},{80,96},{96,112},{112,128},... | collective-permute-start | bytes 983048 | tf_op jit(solution)/shard_map/ppermute | solution.py:201
  203.7 44.2 %collective-permute-start.71 = (f32[128,2048]{1,0:T(8,128)S(1)}, f32[128,2048]{1,0:T(8,128)S(1)}, u32[]{:S(2)}, u32[]{:S(2)}) collective-permute-start(f32[128,2048]{1,0:T(8,128)S(1)} %get-tuple-element.178), channel_id=1, source_target_pairs={{0,240},{16,0},{32,16},{48,32},{64,48},{80,64},{96,80},{112,96},{1... | collective-permute-start | bytes 3145736 | tf_op jit(solution)/shard_map/ppermute | solution.py:201
  231.9 46.3 %collective-permute-start.79 = (f32[128,2048]{1,0:T(8,128)S(1)}, f32[128,2048]{1,0:T(8,128)S(1)}, u32[]{:S(2)}, u32[]{:S(2)}) collective-permute-start(f32[128,2048]{1,0:T(8,128)S(1)} %get-tuple-element.185), channel_id=1, source_target_pairs={{0,240},{16,0},{32,16},{48,32},{64,48},{80,64},{96,80},{112,96},{1... | collective-permute-start | bytes 3145736 | tf_op jit(solution)/shard_map/ppermute | solution.py:201
  232.2 14.2 %collective-permute-start.69 = (f32[8,12288]{1,0:T(8,128)S(1)}, f32[8,12288]{1,0:T(8,128)S(1)}, u32[]{:S(2)}, u32[]{:S(2)}) collective-permute-start(f32[8,12288]{1,0:T(8,128)S(1)} %get-tuple-element.175.refs_0_), channel_id=1, source_target_pairs={{0,16},{16,32},{32,48},{48,64},{64,80},{80,96},{96,112},{112,128},... | collective-permute-start | bytes 1179656 | tf_op jit(solution)/shard_map/ppermute | solution.py:201
  250.1 28.5 %collective-permute-start.78 = (f32[8,14336]{1,0:T(8,128)S(1)}, f32[8,14336]{1,0:T(8,128)S(1)}, u32[]{:S(2)}, u32[]{:S(2)}) collective-permute-start(f32[8,14336]{1,0:T(8,128)S(1)} %get-tuple-element.181.refs_0_), channel_id=1, source_target_pairs={{0,16},{16,32},{32,48},{48,64},{64,80},{80,96},{96,112},{112,128},... | collective-permute-start | bytes 1376264 | tf_op jit(solution)/shard_map/ppermute | solution.py:201
  250.2 13.5 %collective-permute-start.70 = (f32[8,2048]{1,0:T(8,128)S(1)}, f32[8,2048]{1,0:T(8,128)S(1)}, u32[]{:S(2)}, u32[]{:S(2)}) collective-permute-start(f32[8,2048]{1,0:T(8,128)S(1)} %get-tuple-element.176), channel_id=1, source_target_pairs={{0,16},{16,32},{32,48},{48,64},{64,80},{80,96},{96,112},{112,128},... | collective-permute-start | bytes 196616 | tf_op jit(solution)/shard_map/ppermute | solution.py:201
  250.3 13.5 %collective-permute-start.72 = (f32[8,128]{1,0:T(8,128)S(1)}, f32[8,128]{1,0:T(8,128)S(1)}, u32[]{:S(2)}, u32[]{:S(2)}) collective-permute-start(f32[8,128]{1,0:T(8,128)S(1)} %product.37), channel_id=1, source_target_pairs={{0,16},{16,32},{32,48},{48,64},{64,80},{80,96},{96,112},{112,128},... | collective-permute-start | bytes 12296 | tf_op jit(solution)/shard_map/ppermute | solution.py:201
  281.7 25.1 %collective-permute-start.88 = (f32[8,8192]{1,0:T(8,128)S(1)}, f32[8,8192]{1,0:T(8,128)S(1)}, u32[]{:S(2)}, u32[]{:S(2)}) collective-permute-start(f32[8,8192]{1,0:T(8,128)S(1)} %get-tuple-element.189.refs_2_), channel_id=1, source_target_pairs={{0,16},{16,32},{32,48},{48,64},{64,80},{80,96},{96,112},{112,128},... | collective-permute-start | bytes 786440 | tf_op jit(solution)/shard_map/ppermute | solution.py:201
  281.8 9.3 %collective-permute-start.81 = (f32[8,128]{1,0:T(8,128)S(1)}, f32[8,128]{1,0:T(8,128)S(1)}, u32[]{:S(2)}, u32[]{:S(2)}) collective-permute-start(f32[8,128]{1,0:T(8,128)S(1)} %product.39), channel_id=1, source_target_pairs={{0,24},{1,25},{2,26},{3,27},{4,28},{5,29},{6,30},{7,31},{8,16},{9,... | collective-permute-start | bytes 12296 | tf_op jit(solution)/shard_map/ppermute | solution.py:207
  309.7 23.9 %collective-permute-start.97 = (f32[8,8192]{1,0:T(8,128)S(1)}, f32[8,8192]{1,0:T(8,128)S(1)}, u32[]{:S(2)}, u32[]{:S(2)}) collective-permute-start(f32[8,8192]{1,0:T(8,128)S(1)} %get-tuple-element.195.refs_2_), channel_id=1, source_target_pairs={{0,16},{16,32},{32,48},{48,64},{64,80},{80,96},{96,112},{112,128},... | collective-permute-start | bytes 786440 | tf_op jit(solution)/shard_map/ppermute | solution.py:201
  309.8 8.3 %collective-permute-start.89 = (f32[8,128]{1,0:T(8,128)S(1)}, f32[8,128]{1,0:T(8,128)S(1)}, u32[]{:S(2)}, u32[]{:S(2)}) collective-permute-start(f32[8,128]{1,0:T(8,128)S(1)} %product.40), channel_id=1, source_target_pairs={{0,16},{16,32},{32,48},{48,64},{64,80},{80,96},{96,112},{112,128},... | collective-permute-start | bytes 12296 | tf_op jit(solution)/shard_map/ppermute | solution.py:201
  336.5 25.3 %collective-permute-start.106 = (f32[8,8192]{1,0:T(8,128)S(1)}, f32[8,8192]{1,0:T(8,128)S(1)}, u32[]{:S(2)}, u32[]{:S(2)}) collective-permute-start(f32[8,8192]{1,0:T(8,128)S(1)} %get-tuple-element.201.refs_2_), channel_id=1, source_target_pairs={{0,16},{16,32},{32,48},{48,64},{64,80},{80,96},{96,112},{112,128},... | collective-permute-start | bytes 786440 | tf_op jit(solution)/shard_map/ppermute | solution.py:201
  336.6 8.3 %collective-permute-start.98 = (f32[8,128]{1,0:T(8,128)S(1)}, f32[8,128]{1,0:T(8,128)S(1)}, u32[]{:S(2)}, u32[]{:S(2)}) collective-permute-start(f32[8,128]{1,0:T(8,128)S(1)} %product.41), channel_id=1, source_target_pairs={{0,16},{16,32},{32,48},{48,64},{64,80},{80,96},{96,112},{112,128},... | collective-permute-start | bytes 12296 | tf_op jit(solution)/shard_map/ppermute | solution.py:201
  336.6 8.6 %collective-permute-start.99 = (f32[8,128]{1,0:T(8,128)S(1)}, f32[8,128]{1,0:T(8,128)S(1)}, u32[]{:S(2)}, u32[]{:S(2)}) collective-permute-start(f32[8,128]{1,0:T(8,128)S(1)} %product.41), channel_id=1, source_target_pairs={{0,24},{1,25},{2,26},{3,27},{4,28},{5,29},{6,30},{7,31},{8,16},{9,... | collective-permute-start | bytes 12296 | tf_op jit(solution)/shard_map/ppermute | solution.py:207
  353.1 8.7 %collective-permute-start.105 = (f32[8,4096]{1,0:T(8,128)S(1)}, f32[8,4096]{1,0:T(8,128)S(1)}, u32[]{:S(2)}, u32[]{:S(2)}) collective-permute-start(f32[8,4096]{1,0:T(8,128)S(1)} %get-tuple-element.200.refs_1_), channel_id=1, source_target_pairs={{0,16},{16,32},{32,48},{48,64},{64,80},{80,96},{96,112},{112,128},... | collective-permute-start | bytes 393224 | tf_op jit(solution)/shard_map/ppermute | solution.py:201
  364.7 24.5 %collective-permute-start.115 = (f32[8,8192]{1,0:T(8,128)S(1)}, f32[8,8192]{1,0:T(8,128)S(1)}, u32[]{:S(2)}, u32[]{:S(2)}) collective-permute-start(f32[8,8192]{1,0:T(8,128)S(1)} %get-tuple-element.207.refs_2_), channel_id=1, source_target_pairs={{0,16},{16,32},{32,48},{48,64},{64,80},{80,96},{96,112},{112,128},... | collective-permute-start | bytes 786440 | tf_op jit(solution)/shard_map/ppermute | solution.py:201
  364.8 8.3 %collective-permute-start.107 = (f32[8,128]{1,0:T(8,128)S(1)}, f32[8,128]{1,0:T(8,128)S(1)}, u32[]{:S(2)}, u32[]{:S(2)}) collective-permute-start(f32[8,128]{1,0:T(8,128)S(1)} %product.42), channel_id=1, source_target_pairs={{0,16},{16,32},{32,48},{48,64},{64,80},{80,96},{96,112},{112,128},... | collective-permute-start | bytes 12296 | tf_op jit(solution)/shard_map/ppermute | solution.py:201
  380.5 8.7 %collective-permute-start.114 = (f32[8,4096]{1,0:T(8,128)S(1)}, f32[8,4096]{1,0:T(8,128)S(1)}, u32[]{:S(2)}, u32[]{:S(2)}) collective-permute-start(f32[8,4096]{1,0:T(8,128)S(1)} %get-tuple-element.206.refs_1_), channel_id=1, source_target_pairs={{0,16},{16,32},{32,48},{48,64},{64,80},{80,96},{96,112},{112,128},... | collective-permute-start | bytes 393224 | tf_op jit(solution)/shard_map/ppermute | solution.py:201
  392.1 25.2 %collective-permute-start.124 = (f32[8,8192]{1,0:T(8,128)S(1)}, f32[8,8192]{1,0:T(8,128)S(1)}, u32[]{:S(2)}, u32[]{:S(2)}) collective-permute-start(f32[8,8192]{1,0:T(8,128)S(1)} %get-tuple-element.213.refs_2_), channel_id=1, source_target_pairs={{0,16},{16,32},{32,48},{48,64},{64,80},{80,96},{96,112},{112,128},... | collective-permute-start | bytes 786440 | tf_op jit(solution)/shard_map/ppermute | solution.py:201
  392.1 8.3 %collective-permute-start.116 = (f32[8,128]{1,0:T(8,128)S(1)}, f32[8,128]{1,0:T(8,128)S(1)}, u32[]{:S(2)}, u32[]{:S(2)}) collective-permute-start(f32[8,128]{1,0:T(8,128)S(1)} %product.43), channel_id=1, source_target_pairs={{0,16},{16,32},{32,48},{48,64},{64,80},{80,96},{96,112},{112,128},... | collective-permute-start | bytes 12296 | tf_op jit(solution)/shard_map/ppermute | solution.py:201
  392.4 8.4 %collective-permute-start.117 = (f32[8,128]{1,0:T(8,128)S(1)}, f32[8,128]{1,0:T(8,128)S(1)}, u32[]{:S(2)}, u32[]{:S(2)}) collective-permute-start(f32[8,128]{1,0:T(8,128)S(1)} %product.43), channel_id=1, source_target_pairs={{0,24},{1,25},{2,26},{3,27},{4,28},{5,29},{6,30},{7,31},{8,16},{9,... | collective-permute-start | bytes 12296 | tf_op jit(solution)/shard_map/ppermute | solution.py:207
  408.6 8.7 %collective-permute-start.123 = (f32[8,4096]{1,0:T(8,128)S(1)}, f32[8,4096]{1,0:T(8,128)S(1)}, u32[]{:S(2)}, u32[]{:S(2)}) collective-permute-start(f32[8,4096]{1,0:T(8,128)S(1)} %get-tuple-element.212.refs_1_), channel_id=1, source_target_pairs={{0,16},{16,32},{32,48},{48,64},{64,80},{80,96},{96,112},{112,128},... | collective-permute-start | bytes 393224 | tf_op jit(solution)/shard_map/ppermute | solution.py:201
  420.1 24.5 %collective-permute-start.133 = (f32[8,8192]{1,0:T(8,128)S(1)}, f32[8,8192]{1,0:T(8,128)S(1)}, u32[]{:S(2)}, u32[]{:S(2)}) collective-permute-start(f32[8,8192]{1,0:T(8,128)S(1)} %get-tuple-element.219.refs_2_), channel_id=1, source_target_pairs={{0,16},{16,32},{32,48},{48,64},{64,80},{80,96},{96,112},{112,128},... | collective-permute-start | bytes 786440 | tf_op jit(solution)/shard_map/ppermute | solution.py:201
  420.2 8.3 %collective-permute-start.125 = (f32[8,128]{1,0:T(8,128)S(1)}, f32[8,128]{1,0:T(8,128)S(1)}, u32[]{:S(2)}, u32[]{:S(2)}) collective-permute-start(f32[8,128]{1,0:T(8,128)S(1)} %product.44), channel_id=1, source_target_pairs={{0,16},{16,32},{32,48},{48,64},{64,80},{80,96},{96,112},{112,128},... | collective-permute-start | bytes 12296 | tf_op jit(solution)/shard_map/ppermute | solution.py:201
  435.9 8.7 %collective-permute-start.132 = (f32[8,4096]{1,0:T(8,128)S(1)}, f32[8,4096]{1,0:T(8,128)S(1)}, u32[]{:S(2)}, u32[]{:S(2)}) collective-permute-start(f32[8,4096]{1,0:T(8,128)S(1)} %get-tuple-element.218.refs_1_), channel_id=1, source_target_pairs={{0,16},{16,32},{32,48},{48,64},{64,80},{80,96},{96,112},{112,128},... | collective-permute-start | bytes 393224 | tf_op jit(solution)/shard_map/ppermute | solution.py:201
  447.5 25.2 %collective-permute-start.142 = (f32[8,8192]{1,0:T(8,128)S(1)}, f32[8,8192]{1,0:T(8,128)S(1)}, u32[]{:S(2)}, u32[]{:S(2)}) collective-permute-start(f32[8,8192]{1,0:T(8,128)S(1)} %get-tuple-element.225.refs_2_), channel_id=1, source_target_pairs={{0,16},{16,32},{32,48},{48,64},{64,80},{80,96},{96,112},{112,128},... | collective-permute-start | bytes 786440 | tf_op jit(solution)/shard_map/ppermute | solution.py:201
  447.6 8.6 %collective-permute-start.135 = (f32[8,128]{1,0:T(8,128)S(1)}, f32[8,128]{1,0:T(8,128)S(1)}, u32[]{:S(2)}, u32[]{:S(2)}) collective-permute-start(f32[8,128]{1,0:T(8,128)S(1)} %product.45), channel_id=1, source_target_pairs={{0,24},{1,25},{2,26},{3,27},{4,28},{5,29},{6,30},{7,31},{8,16},{9,... | collective-permute-start | bytes 12296 | tf_op jit(solution)/shard_map/ppermute | solution.py:207
  464.0 8.7 %collective-permute-start.141 = (f32[8,4096]{1,0:T(8,128)S(1)}, f32[8,4096]{1,0:T(8,128)S(1)}, u32[]{:S(2)}, u32[]{:S(2)}) collective-permute-start(f32[8,4096]{1,0:T(8,128)S(1)} %get-tuple-element.224.refs_1_), channel_id=1, source_target_pairs={{0,16},{16,32},{32,48},{48,64},{64,80},{80,96},{96,112},{112,128},... | collective-permute-start | bytes 393224 | tf_op jit(solution)/shard_map/ppermute | solution.py:201
  474.1 13.9 %collective-permute-start.145 = (f32[8,8192]{1,0:T(8,128)S(1)}, f32[8,8192]{1,0:T(8,128)S(1)}, u32[]{:S(2)}, u32[]{:S(2)}) collective-permute-start(f32[8,8192]{1,0:T(8,128)S(1)} %get-tuple-element.228), channel_id=1, source_target_pairs={{0,16},{16,32},{32,48},{48,64},{64,80},{80,96},{96,112},{112,128},... | collective-permute-start | bytes 786440 | tf_op jit(solution)/shard_map/ppermute | solution.py:201
  474.2 11.0 %collective-permute-start.144 = (f32[8,4096]{1,0:T(8,128)S(1)}, f32[8,4096]{1,0:T(8,128)S(1)}, u32[]{:S(2)}, u32[]{:S(2)}) collective-permute-start(f32[8,4096]{1,0:T(8,128)S(1)} %get-tuple-element.227), channel_id=1, source_target_pairs={{0,16},{16,32},{32,48},{48,64},{64,80},{80,96},{96,112},{112,128},... | collective-permute-start | bytes 393224 | tf_op jit(solution)/shard_map/ppermute | solution.py:201
  474.3 13.7 %collective-permute-start.143 = (f32[8,4096]{1,0:T(8,128)S(1)}, f32[8,4096]{1,0:T(8,128)S(1)}, u32[]{:S(2)}, u32[]{:S(2)}) collective-permute-start(f32[8,4096]{1,0:T(8,128)S(1)} %get-tuple-element.226), channel_id=1, source_target_pairs={{0,16},{16,32},{32,48},{48,64},{64,80},{80,96},{96,112},{112,128},... | collective-permute-start | bytes 393224 | tf_op jit(solution)/shard_map/ppermute | solution.py:201
  (101 other events, 487.5 us)
